TPU v7x, 512 devices: a whole 4x8x8 slice. The times are simulated.
512 devices in a mesh: tensor: 8 (over x, core), dp: 64 (over y, z).
Axes of the slice: x: 4, y: 8, z: 8, core: 2. Of those that a mesh axis runs over, the one named last changes fastest.
Arguments:
- inputs: bfloat16 [16384, 8192], P('dp', 'tensor'), may hold values from -6 to 6
- frozen_value_weight: bfloat16 [8192, 1024], P(None, 'tensor'), may hold values from -0.0625 to 0.0625
- adapter_down_matrix: bfloat16 [64, 8192, 16], P('dp', 'tensor'), may hold values from -0.0625 to 0.0625
- adapter_up_matrix: bfloat16 [64, 16, 1024], P('dp', None, 'tensor'), may hold values from -1.5 to 1.5
- value_cotangent: bfloat16 [16384, 1024], P('dp', 'tensor'), may hold values from -6 to 6
- tenant_of_block: int32 [128], P('dp'), may hold values from 0 to 63
- quotas: int32 [64], replicated, may hold values from 128 to 1023
Outputs:
- adapted_values: bfloat16 [16384, 1024], P('dp', 'tensor')
- gradient_inputs: bfloat16 [16384, 8192], P('dp', 'tensor')
- down_grad: float32 [64, 8192, 16], P('dp', 'tensor')
- gradient_up_matrix: float32 [64, 16, 1024], P('dp', None, 'tensor')
All inputs are finite; a program needn't handle non-finite values.
Results may differ from a plain program's by a relative error of at most 0.015.
Values may be sent and summed in bfloat16 or wider, within the bound.
A program may use at most 64 MiB of HBM per device.

v0:
```python
import jax
import jax.numpy as jnp
from jax import lax
from jax.sharding import PartitionSpec as P

ADAPTER_RANK = 16
BLOCK = 128


adapter_scale = 2.0


def cut_along(value, dim, length):
    before, after = (value.shape[:dim], value.shape[dim + 1 :])
    return jnp.moveaxis(value.reshape(*before, length, -1, *after), dim, 0)


def sum_at_owner(value, axis, dim):
    length = lax.axis_size(axis)
    blocks = lax.all_to_all(cut_along(value, dim, length), axis, 0, 0, tiled=True)
    return jnp.sum(blocks.astype(jnp.float32), axis=0)


def laid_out(blocks, dim):
    blocks = jnp.moveaxis(blocks, 0, dim)
    shape = blocks.shape
    return blocks.reshape(*shape[:dim], shape[dim] * shape[dim + 1], *shape[dim + 2 :])


def sent_to_all(value, axis):
    copies = jnp.broadcast_to(value, (lax.axis_size(axis), *value.shape))
    return lax.all_to_all(copies, axis, split_axis=0, concat_axis=0, tiled=True)


def gather_directly(value, axis, dim):
    return laid_out(sent_to_all(value, axis), dim)


def sent_together(arrays, axis, dim, along):
    columns = [a.reshape(*a.shape[:along], -1) for a in arrays]
    both = jnp.concatenate(columns, axis=along)
    whole, at, outs = (lax.all_gather(both, axis, axis=dim, tiled=True), 0, [])
    for a, column in zip(arrays, columns):
        section = whole[..., at : at + column.shape[along]]
        outs.append(section.reshape(*section.shape[:along], *a.shape[along:]))
        at += column.shape[along]
    return tuple(outs)


def on_device(
    inputs,
    frozen_value_weight,
    adapter_down_matrix,
    adapter_up_matrix,
    value_cotangent,
    tenant_of_block,
    quotas,
):
    token_rows, local_features = inputs.shape
    local_values = frozen_value_weight.shape[1]
    nblocks = tenant_of_block.shape[0]
    owned_adapters = adapter_down_matrix.shape[0]
    adapter_count = owned_adapters * lax.axis_size("dp")
    groups = lax.axis_size("tensor")
    weight_rows = lax.all_to_all(
        frozen_value_weight, "tensor", split_axis=0, concat_axis=1, tiled=True
    )
    base_terms = jnp.dot(inputs, weight_rows, preferred_element_type=jnp.float32)
    frozen_output = sum_at_owner(base_terms.astype(jnp.bfloat16), "tensor", 1)
    grad_full = gather_directly(value_cotangent, "tensor", 1)
    summed_gradient = jnp.zeros((token_rows, local_features), jnp.float32)
    for index in range(groups):
        lower = index * local_values
        term = lax.dot_general(
            grad_full[:, lower : lower + local_values],
            weight_rows[:, lower : lower + local_values],
            (((1,), (1,)), ((), ())),
            preferred_element_type=jnp.float32,
        )
        summed_gradient = summed_gradient + term.astype(jnp.bfloat16).astype(jnp.float32)
    tenant_all = gather_directly(tenant_of_block, "dp", 0)
    down_all, up_all = (
        lax.all_gather(adapter_down_matrix, "dp", axis=0, tiled=True),
        lax.all_gather(adapter_up_matrix, "dp", axis=0, tiled=True),
    )
    down_blocks = down_all[tenant_of_block]
    up_blocks = up_all[tenant_of_block]
    input_blocks = inputs.reshape(nblocks, BLOCK, local_features)
    value_grad_blocks = value_cotangent.reshape(nblocks, BLOCK, local_values)
    low_part = jnp.einsum(
        "bnd,bdr->bnr", input_blocks, down_blocks, preferred_element_type=jnp.float32
    )
    gradient_portion = adapter_scale * jnp.einsum(
        "bnk,brk->bnr", value_grad_blocks, up_blocks, preferred_element_type=jnp.float32
    )
    low_sum, grad_sum = (
        lax.psum(low_part.astype(jnp.bfloat16), "tensor").astype(jnp.float32),
        lax.psum(gradient_portion.astype(jnp.bfloat16), "tensor").astype(jnp.float32),
    )
    reduced_features = low_sum.astype(jnp.bfloat16)
    gradient_lowrank = grad_sum.astype(jnp.bfloat16)
    raised_output = jnp.einsum(
        "bnr,brk->bnk", reduced_features, up_blocks, preferred_element_type=jnp.float32
    )
    adapted_values = (
        frozen_output + adapter_scale * raised_output.reshape(token_rows, local_values)
    ).astype(jnp.bfloat16)
    adapter_input = jnp.einsum(
        "bnr,bdr->bnd", gradient_lowrank, down_blocks, preferred_element_type=jnp.float32
    )
    gradient_inputs = (summed_gradient + adapter_input.reshape(token_rows, local_features)).astype(
        jnp.bfloat16
    )
    adapter_ids = jnp.arange(adapter_count, dtype=jnp.int32)
    counts = (
        jnp.sum((tenant_all[:, None] == adapter_ids[None, :]).astype(jnp.float32), axis=0) * BLOCK
    )
    scale = quotas.astype(jnp.float32) / jnp.maximum(counts, 1.0)
    local_hot = (tenant_of_block[:, None] == adapter_ids[None, :]).astype(jnp.float32)
    block_weight = jnp.dot(local_hot, scale, precision=lax.Precision.HIGHEST)
    grad_a = (
        jnp.einsum(
            "bnd,bnr->bdr", input_blocks, gradient_lowrank, preferred_element_type=jnp.float32
        )
        * block_weight[:, None, None]
    )
    up_gradient_local = (
        adapter_scale
        * jnp.einsum(
            "bnr,bnk->brk", reduced_features, value_grad_blocks, preferred_element_type=jnp.float32
        )
        * block_weight[:, None, None]
    )
    my_index = lax.axis_index("dp")
    first_owned = my_index * owned_adapters
    owned_ids = first_owned + jnp.arange(owned_adapters, dtype=jnp.int32)
    start_a = jnp.zeros((owned_adapters, local_features, ADAPTER_RANK), jnp.float32)
    start_b = jnp.zeros((owned_adapters, ADAPTER_RANK, local_values), jnp.float32)
    pieces = tuple(
        (
            part.astype(jnp.float32)
            for part in sent_together(
                (grad_a.astype(jnp.bfloat16), up_gradient_local.astype(jnp.bfloat16)), "dp", 0, 1
            )
        )
    )
    selector = (tenant_all[:, None] == owned_ids[None, :]).astype(jnp.float32)
    new_a = start_a + jnp.einsum(
        "bo,bdr->odr", selector, pieces[0], precision=lax.Precision.HIGHEST
    )
    new_b = start_b + jnp.einsum(
        "bo,brk->ork", selector, pieces[1], precision=lax.Precision.HIGHEST
    )
    return (adapted_values, gradient_inputs, new_a, new_b)


def solution(mesh):
    placed = (
        P("dp", "tensor"),
        P(None, "tensor"),
        P("dp", "tensor", None),
        P("dp", None, "tensor"),
        P("dp", "tensor"),
        P("dp"),
        P(),
    )
    return jax.shard_map(
        on_device,
        mesh=mesh,
        in_specs=placed,
        out_specs=(
            P("dp", "tensor"),
            P("dp", "tensor"),
            P("dp", "tensor", None),
            P("dp", None, "tensor"),
        ),
        check_vma=False,
    )
```

profile of v0, /device:TPU:1, one launch (start us, length us, event | category | flops | bytes accessed | tf_op | source)
XLA Modules:
  0.0 246.2 jit_solution(11249866176702770566)
XLA Ops:
  7.9 1.3 broadcast_in_dim.8
  9.2 17.1 %all-to-all-start.3 = ((s32[64,1,2]{2,1,0:T(1,128)}), s32[64,1,2]{2,1,0:T(1,128)S(1)}, u32[]{:S(2)}, u32[]{:S(2)}) async-start(s32[64,1,2]{2,1,0:T(1,128)} %broadcast_in_dim.8), calls=%async_computation.3 | async-start | bytes 65536 | tf_op jit(solution)/shard_map/all_to_all | solution.py:32
  26.4 39.9 %all_gather.10 = bf16[64,16,128]{2,1,0:T(8,128)(2,1)S(1)} all-gather(bf16[1,16,128]{2,1,0:T(8,128)(2,1)} %param.10), channel_id=1, replica_groups=mesh['tensor'=8,'dp'=64] {'dp'}, dimensions={0}, use_global_device_ids=true | all-gather | bytes 266240 | tf_op jit(solution)/shard_map/all_gather | solution.py:84
  67.5 1.0 fusion.23
  70.9 25.0 %all-gather.4.cloned.1.call-done = bf16[64,1024,16]{1,2,0:T(8,128)(2,1)} async-done(((bf16[1,1024,16]{1,2,0:T(8,128)(2,1)}), bf16[64,1024,16]{1,2,0:T(8,128)(2,1)}) %all-gather.4.cloned.1.call-update) | async-done | bytes 2097168 | tf_op jit(solution)/shard_map/all_gather | solution.py:83
  95.9 2.1 gather_fusion
  98.3 25.0 %all-reduce = (bf16[2,128,16]{1,2,0:T(8,128)(2,1)S(1)}, bf16[2,128,16]{1,2,0:T(8,128)(2,1)S(1)}) all-reduce(bf16[2,128,16]{1,2,0:T(8,128)(2,1)S(1)} %fusion.24, bf16[2,128,16]{1,2,0:T(8,128)(2,1)S(1)} %fusion.23), channel_id=1, replica_groups=mesh['tensor'=8,'dp'=64] {'tensor'}, use_global_device_ids=true, to_apply=%region_1.0 | all-reduce | flops 8192 | bytes 32768 | tf_op jit(solution)/shard_map/psum | solution.py:97
  125.1 7.1 %all-to-all-start = ((bf16[8,1024,128]{2,1,0:T(8,128)(2,1)}), bf16[8,1024,128]{2,1,0:T(8,128)(2,1)S(1)}, u32[]{:S(2)}, u32[]{:S(2)}) async-start(bf16[8,1024,128]{2,1,0:T(8,128)(2,1)} %bitcast.84), calls=%async_computation | async-start | bytes 4194304 | tf_op jit(solution)/shard_map/all_to_all | solution.py:65
  132.3 26.1 %all-to-all-done = bf16[8,1024,128]{2,1,0:T(8,128)(2,1)S(1)} async-done(((bf16[8,1024,128]{2,1,0:T(8,128)(2,1)}), bf16[8,1024,128]{2,1,0:T(8,128)(2,1)S(1)}, u32[]{:S(2)}, u32[]{:S(2)}) %all-to-all-start) | async-done | bytes 2097184 | tf_op jit(solution)/shard_map/all_to_all | solution.py:65
  159.3 4.4 %all-to-all-start.2 = ((bf16[8,256,128]{1,2,0:T(8,128)(2,1)}), bf16[8,256,128]{1,2,0:T(8,128)(2,1)S(1)}, u32[]{:S(2)}, u32[]{:S(2)}) async-start(bf16[8,256,128]{1,2,0:T(8,128)(2,1)} %broadcast_in_dim.7), calls=%async_computation.2 | async-start | bytes 1048576 | tf_op jit(solution)/shard_map/all_to_all | solution.py:32
  163.9 2.9 %copy.28 = bf16[1024,8,128]{0,2,1:T(8,128)(2,1)S(1)} copy(bf16[1024,8,128]{2,0,1:T(8,128)(2,1)} %bitcast.82) | data formatting | bytes 4194304 | tf_op jit(solution)/shard_map/all_to_all | solution.py:65
  168.5 4.6 %all-to-all-done.2 = bf16[8,256,128]{1,2,0:T(8,128)(2,1)S(1)} async-done(((bf16[8,256,128]{1,2,0:T(8,128)(2,1)}), bf16[8,256,128]{1,2,0:T(8,128)(2,1)S(1)}, u32[]{:S(2)}, u32[]{:S(2)}) %all-to-all-start.2) | async-done | bytes 524320 | tf_op jit(solution)/shard_map/all_to_all | solution.py:32
  173.8 4.4 %all-to-all-start.1 = ((bf16[8,256,128]{2,1,0:T(8,128)(2,1)}), bf16[8,256,128]{2,1,0:T(8,128)(2,1)S(1)}, u32[]{:S(2)}, u32[]{:S(2)}) async-start(bf16[8,256,128]{2,1,0:T(8,128)(2,1)} %bitcast.93), calls=%async_computation.1 | async-start | bytes 1048576 | tf_op jit(solution)/shard_map/all_to_all | solution.py:20
  178.2 1.2 fusion.16
  179.4 1.2 fusion.15
  181.9 1.3 fusion.5
  183.2 4.4 %all-to-all-done.1 = bf16[8,256,128]{2,1,0:T(8,128)(2,1)S(1)} async-done(((bf16[8,256,128]{2,1,0:T(8,128)(2,1)}), bf16[8,256,128]{2,1,0:T(8,128)(2,1)S(1)}, u32[]{:S(2)}, u32[]{:S(2)}) %all-to-all-start.1) | async-done | bytes 524320 | tf_op jit(solution)/shard_map/all_to_all | solution.py:20
  188.9 2.0 fusion.3
  190.8 15.3 %all-gather.6.cloned.1.call-done = bf16[64,2,18432]{2,1,0:T(2,128)(2,1)} async-done(((bf16[1,2,18432]{2,1,0:T(2,128)(2,1)}), bf16[64,2,18432]{2,1,0:T(2,128)(2,1)}) %all-gather.6.cloned.1.call-update) | async-done | bytes 4718608 | tf_op jit(solution)/shard_map/all_gather | solution.py:42
  206.2 7.6 %reshape.94 = bf16[128,18432]{1,0:T(8,128)(2,1)} reshape(bf16[64,2,18432]{2,1,0:T(2,128)(2,1)} %all-gather.6.cloned.1.call-done) | data formatting | bytes 9437184
  213.7 4.5 %slice.92 = bf16[128,16384]{1,0:T(8,128)(2,1)} slice(bf16[128,18432]{1,0:T(8,128)(2,1)} %reshape.94), slice={[0:128], [0:16384]} | slice | bytes 8388608 | tf_op jit(solution)/shard_map/slice | solution.py:44
  218.2 1.8 fusion.25
  220.0 6.4 %copy.32 = bf16[128,16384]{0,1:T(8,128)(2,1)} copy(bf16[128,16384]{1,0:T(8,128)(2,1)} %slice.92) | data formatting | bytes 8388608 | tf_op jit(solution)/shard_map/slice | solution.py:44
  226.5 12.0 %fusion.55 = f32[1,1024,16]{2,0,1:T(1,128)S(1)} fusion(pred[128,1,1]{0,1,2:T(4,128)(4,1)S(1)} %reshape.97, bf16[128,1024,16]{0,2,1:T(8,128)(2,1)} %bitcast.72), kind=kOutput, calls=%fused_computation.84 | convolution fusion | flops 4194304 | bytes 4259968 | tf_op jit(solution)/shard_map/bo,bdr->odr/dot_general | solution.py:148
  (47 shorter events, 13.6 us)
Async XLA Ops:
  7.2 90.9 %copy-start = (bf16[256,1024]{1,0:T(8,128)(2,1)S(1)}, bf16[256,1024]{1,0:T(8,128)(2,1)}, u32[]{:S(2)}) copy-start(bf16[256,1024]{1,0:T(8,128)(2,1)} %param.7) | copy-start | bytes 1572868
  7.2 116.1 %copy-start.5 = (bf16[256,128]{1,0:T(8,128)(2,1)S(1)}, bf16[256,128]{1,0:T(8,128)(2,1)}, u32[]{:S(2)}) copy-start(bf16[256,128]{1,0:T(8,128)(2,1)} %param.11) | copy-start | bytes 196612
  7.2 88.7 %all-gather.4.cloned.1.call-start = ((), (), s32[]{:S(2)}) async-start(), calls=%async_computation.4 | async-start | bytes 2129920 | tf_op jit(solution)/shard_map/all_gather | solution.py:83
  9.2 59.3 %all-to-all-start.3 = ((s32[64,1,2]{2,1,0:T(1,128)}), s32[64,1,2]{2,1,0:T(1,128)S(1)}, u32[]{:S(2)}, u32[]{:S(2)}) async-start(s32[64,1,2]{2,1,0:T(1,128)} %broadcast_in_dim.8), calls=%async_computation.3 | async-start | bytes 65536 | tf_op jit(solution)/shard_map/all_to_all | solution.py:32
  26.3 179.8 %all-gather.6.cloned.1.call-start = ((), (), s32[]{:S(2)}) async-start(), calls=%async_computation.5 | async-start | bytes 4792320 | tf_op jit(solution)/shard_map/all_gather | solution.py:42
  125.1 33.3 %all-to-all-start = ((bf16[8,1024,128]{2,1,0:T(8,128)(2,1)}), bf16[8,1024,128]{2,1,0:T(8,128)(2,1)S(1)}, u32[]{:S(2)}, u32[]{:S(2)}) async-start(bf16[8,1024,128]{2,1,0:T(8,128)(2,1)} %bitcast.84), calls=%async_computation | async-start | bytes 4194304 | tf_op jit(solution)/shard_map/all_to_all | solution.py:65
  158.4 5.5 %copy-start.1 = (bf16[8,1024,128]{2,1,0:T(8,128)(2,1)}, bf16[8,1024,128]{2,1,0:T(8,128)(2,1)S(1)}, u32[]{:S(2)}) copy-start(bf16[8,1024,128]{2,1,0:T(8,128)(2,1)S(1)} %all-to-all-done) | copy-start | bytes 6291460
  159.3 13.7 %all-to-all-start.2 = ((bf16[8,256,128]{1,2,0:T(8,128)(2,1)}), bf16[8,256,128]{1,2,0:T(8,128)(2,1)S(1)}, u32[]{:S(2)}, u32[]{:S(2)}) async-start(bf16[8,256,128]{1,2,0:T(8,128)(2,1)} %broadcast_in_dim.7), calls=%async_computation.2 | async-start | bytes 1048576 | tf_op jit(solution)/shard_map/all_to_all | solution.py:32
  173.1 0.8 copy-start.3
  173.8 13.7 %all-to-all-start.1 = ((bf16[8,256,128]{2,1,0:T(8,128)(2,1)}), bf16[8,256,128]{2,1,0:T(8,128)(2,1)S(1)}, u32[]{:S(2)}, u32[]{:S(2)}) async-start(bf16[8,256,128]{2,1,0:T(8,128)(2,1)} %bitcast.93), calls=%async_computation.1 | async-start | bytes 1048576 | tf_op jit(solution)/shard_map/all_to_all | solution.py:20
  178.2 2.4 copy-start.4
  187.6 1.3 copy-start.2
Sparse Core Ops, SparseCore 0:
  11.0 84.8 all-gather.3
  125.2 80.8 all-gather.5
where the time goes:
time: 250 us; the launch traced here: 246 us
  waiting for transfers between devices  76.1 us (30%)
  blocking collectives  64.9 us (26%)
  starting transfers between devices  33 us (13%)
  local copies, waits for them, and re-layouts  30.6 us (12%)
  matrix products  24.4 us (10%)
  between operations  14.2 us (6%)
  other arithmetic  3.02 us (1%)
    all_gather x1, blocking collectives, on_device(): lax.all_gather(adapter_up_matrix, 'dp', axis=0, tiled=True)  39.9 us
    all_to_all x1, waiting for transfers between devices, on_device(): lax.all_to_all(frozen_value_weight, 'tensor', split_axis=0, concat_axis=1...  26.1 us
    all_gather x1, waiting for transfers between devices, on_device(): lax.all_gather(adapter_down_matrix, 'dp', axis=0, tiled=True)  25 us
    psum x1, blocking collectives, on_device(): lax.psum(low_part.astype(jnp.bfloat16), 'tensor').astype(jnp.float32)  25 us
    all_to_all x2, starting transfers between devices, sent_to_all(): return lax.all_to_all(copies, axis, split_axis=0, concat_axis=0, tiled=True)  21.5 us
    all_gather x1, waiting for transfers between devices, sent_together(): whole, at, outs = (lax.all_gather(both, axis, axis=dim, tiled=True), 0, [])  15.3 us
    dot_general x1, matrix products, on_device(): jnp.einsum('bo,bdr->odr', selector, pieces[0], precision=lax.Precision.HI...  12 us
    slice x2, local copies, waits for them, and re-layouts, sent_together(): section = whole[..., at:at + column.shape[along]]  10.9 us
  transfers between devices with their start and end apart: 6, of which 5 were waited for; matrix products, arithmetic and copies ran while one was open for 8% of the time, Pallas kernels for 0%

commit v1 on v0

v1 whole, which is shorter than its diff:
```python
import functools

import jax
import jax.numpy as jnp
from jax import lax
from jax.experimental import pallas as pl
from jax.experimental.pallas import tpu as pltpu
from jax.sharding import PartitionSpec as P

MESH = pl.DeviceIdType.MESH
BLOCK = 128
LINE = 8
ADAPTER_SCALE = 2.0
BF16 = jnp.bfloat16
F32 = jnp.float32

TZ, TY, AZ, AY, SY, SZ, VAL, WGT, RANK, BASE, GZ, GY, HY, HZ, CNT = range(15)


def far_first(n):
    return sorted(range(1, n), key=lambda off: (-min(off, n - off), off))


def nt_dot(a, b):
    return lax.dot_general(a, b, (((1,), (1,)), ((), ())), preferred_element_type=F32)


def tn_dot(a, b):
    return lax.dot_general(a, b, (((0,), (0,)), ((), ())), preferred_element_type=F32)


def kernel(
    nt, ny, nz,
    ten_s, quo_s, x_hbm, w_hbm, a_hbm, b_hbm, v_hbm,
    out_ref, gin_hbm, da_ref, db_ref,
    tile, tz_v, ty_v, tz_s, ty_s, all_ten,
    xv, a1, a2, row1, col2, s1, s2, r1, r2,
    vbuf, wbuf, pbuf, bsend, ebuf, g1, g2, gz_v, gy_v, h1, h2, hz1, hz2, gin_v,
    loc, ss, rs,
):
    t = lax.axis_index("tensor")
    d = lax.axis_index("dp")
    y, z = lax.div(d, nz), lax.rem(d, nz)
    rows, feats = xv.shape
    nb = rows // BLOCK
    half = a2.shape[1]
    first = feats - half
    values = v_hbm.shape[1]
    rank = a2.shape[0]

    lines = {
        "t": (t, nt, lambda p: {"tensor": p}),
        "y": (y, ny, lambda p: {"dp": p * nz + z}),
        "z": (z, nz, lambda p: {"dp": y * nz + p}),
    }

    def remote(kind, line, src, dst, peer):
        me, _, dev = lines[line]
        return pltpu.make_async_remote_copy(
            src_ref=src, dst_ref=dst, send_sem=ss.at[kind, peer], recv_sem=rs.at[kind, me],
            device_id=dev(peer), device_id_type=MESH,
        )

    def arrived(kind, line, buf, peer):
        _, _, dev = lines[line]
        pltpu.make_async_remote_copy(
            src_ref=buf.at[peer], dst_ref=buf.at[peer], send_sem=ss.at[kind, peer],
            recv_sem=rs.at[kind, peer], device_id=dev(peer), device_id_type=MESH,
        ).wait_recv()

    def peers(line, fn):
        me, n, _ = lines[line]
        for off in far_first(n):
            fn(lax.rem(me + off, n))

    def each(line, fn):
        me, n, _ = lines[line]

        def body(off, carry):
            fn(lax.rem(me + off, n))
            return carry

        lax.fori_loop(1, n, body, 0)

    local = [
        pltpu.make_async_copy(a_hbm.at[:, pl.ds(0, first)], a1.at[:, pl.ds(0, first)], loc.at[0]),
        pltpu.make_async_copy(b_hbm, a1.at[:, pl.ds(first, values)], loc.at[1]),
        pltpu.make_async_copy(a_hbm.at[:, pl.ds(first, half)], a2, loc.at[2]),
        pltpu.make_async_copy(x_hbm, xv, loc.at[3]),
        pltpu.make_async_copy(v_hbm, vbuf.at[t], loc.at[4]),
        pltpu.make_async_copy(w_hbm.at[pl.ds(t * feats, feats)], wbuf.at[t], loc.at[5]),
    ]
    for copy in local:
        copy.start()
    lane = lax.broadcasted_iota(jnp.int32, tile.shape, 1)
    mine = jnp.full(tile.shape, -1, jnp.int32)
    for k in range(nb):
        mine = jnp.where(lane == k, ten_s[k], mine)
    tile[...] = mine
    tz_v[z] = mine
    ty_v[y] = mine

    barrier = pltpu.get_barrier_semaphore()
    for line in ("t", "y", "z"):
        dev = lines[line][2]
        each(line, lambda p: pl.semaphore_signal(barrier, inc=1, device_id=dev(p), device_id_type=MESH))
    local[0].wait()
    local[1].wait()
    local[2].wait()
    row1[z] = a1[...]
    col2[y] = a2[...]
    pl.semaphore_wait(barrier, nt + ny + nz - 3)

    peers("z", lambda p: remote(TZ, "z", tile, tz_v.at[z], p).start())
    peers("y", lambda p: remote(TY, "y", tile, ty_v.at[y], p).start())
    peers("z", lambda p: remote(AZ, "z", a1, row1.at[z], p).start())
    peers("y", lambda p: remote(AY, "y", a2, col2.at[y], p).start())
    peers("t", lambda p: remote(WGT, "t", w_hbm.at[pl.ds(p * feats, feats)], wbuf.at[t], p).start())
    local[4].wait()
    peers("t", lambda p: remote(VAL, "t", vbuf.at[t], vbuf.at[t], p).start())

    each("z", lambda p: arrived(TZ, "z", tz_v, p))
    each("y", lambda p: arrived(TY, "y", ty_v, p))
    to_z = pltpu.make_async_copy(tz_v, tz_s, loc.at[0])
    to_y = pltpu.make_async_copy(ty_v, ty_s, loc.at[1])
    to_z.start()
    to_y.start()
    all_ten[y] = tz_v[...]
    to_z.wait()
    to_y.wait()
    each("z", lambda p: arrived(AZ, "z", row1, p))

    def pick1(p, to):
        for k in range(nb):
            to[k] = row1[lax.rem(ty_s[p, 0, k], nz)]

    def send1(p):
        pick1(p, s1.at[p])
        remote(SY, "y", s1.at[p], r1.at[y], p).start()

    peers("y", send1)
    pick1(y, r1.at[y])
    each("y", lambda p: arrived(AY, "y", col2, p))

    def pick2(p, to):
        for k in range(nb):
            to[k] = col2[lax.div(tz_s[p, 0, k], nz)]

    def send2(p):
        pick2(p, s2.at[p])
        remote(SZ, "z", s2.at[p], r2.at[z], p).start()

    peers("z", send2)
    pick2(z, r2.at[z])
    peers("y", lambda p: remote(CNT, "y", tz_v, all_ten.at[y], p).start())

    local[3].wait()
    local[5].wait()
    each("y", lambda p: arrived(SY, "y", r1, p))
    each("z", lambda p: arrived(SZ, "z", r2, p))

    first_at, second_at, up_at = [], [], []
    for k in range(nb):
        tenant = ten_s[k]
        part1 = r1[lax.div(tenant, nz), k]
        at2 = r2[lax.rem(tenant, nz), k]
        at1, up = part1[:, :first], part1[:, first:]
        first_at.append(at1)
        second_at.append(at2)
        up_at.append(up)
        span = pl.ds(k * BLOCK, BLOCK)
        low = nt_dot(at1, xv[span, :first]) + nt_dot(at2, xv[span, first:])
        grad = ADAPTER_SCALE * nt_dot(up, vbuf[t, span, :])
        pbuf[t, :rank, span] = low.astype(BF16)
        pbuf[t, rank:, span] = grad.astype(BF16)
    peers("t", lambda p: remote(RANK, "t", pbuf.at[t], pbuf.at[t], p).start())
    each("t", lambda p: arrived(RANK, "t", pbuf, p))
    total = pbuf[0].astype(F32)
    for j in range(1, nt):
        total = total + pbuf[j].astype(F32)
    low_t, grad_t = total[:rank].astype(BF16), total[rank:].astype(BF16)

    for k in range(nb):
        span = slice(k * BLOCK, (k + 1) * BLOCK)
        low_k, grad_k = low_t[:, span], grad_t[:, span]
        g1[k, :, :first] = jnp.dot(grad_k, xv[span, :first], preferred_element_type=F32).astype(BF16)
        g1[k, :, first:] = (
            ADAPTER_SCALE * jnp.dot(low_k, vbuf[t, span, :], preferred_element_type=F32)
        ).astype(BF16)
        g2[k] = jnp.dot(grad_k, xv[span, first:], preferred_element_type=F32).astype(BF16)
    peers("z", lambda p: remote(GZ, "z", g1, gz_v.at[z], p).start())
    peers("y", lambda p: remote(GY, "y", g2, gy_v.at[y], p).start())
    gz_v[z] = g1[...]
    gy_v[y] = g2[...]

    def base_of(p):
        return jnp.dot(xv[...], wbuf[p], preferred_element_type=F32).astype(BF16)

    ebuf[t] = base_of(t)

    def send_base(p):
        arrived(WGT, "t", wbuf, p)
        bsend[p] = base_of(p)
        remote(BASE, "t", bsend.at[p], ebuf.at[t], p).start()

    each("t", send_base)

    each("t", lambda p: arrived(VAL, "t", vbuf, p))
    tiles = 4
    width = feats // tiles
    for i in range(tiles):
        cols = slice(i * width, (i + 1) * width)
        acc = nt_dot(vbuf[0], wbuf[0, cols, :])
        for j in range(1, nt):
            acc = acc + nt_dot(vbuf[j], wbuf[j, cols, :])
        for k in range(nb):
            span = slice(k * BLOCK, (k + 1) * BLOCK)
            if (i + 1) * width <= first:
                at = first_at[k][:, cols]
            else:
                at = second_at[k][:, i * width - first : (i + 1) * width - first]
            gin_v[span, cols] = (acc[span] + tn_dot(grad_t[:, span], at)).astype(BF16)
    gin_copy = pltpu.make_async_copy(gin_v, gin_hbm, loc.at[2])
    gin_copy.start()

    each("z", lambda p: arrived(GZ, "z", gz_v, p))

    def sum1(p, to):
        owner = p * nz + z
        acc = jnp.zeros(g1.shape[1:], F32)
        for j in range(nz):
            for k in range(nb):
                hit = jnp.where(tz_s[j, 0, k] == owner, 1.0, 0.0).astype(F32)
                acc = acc + hit * gz_v[j, k].astype(F32)
        to[...] = acc.astype(BF16)

    def send_sum1(p):
        sum1(p, h1.at[p])
        remote(HY, "y", h1.at[p], hz1.at[y], p).start()

    each("y", send_sum1)
    sum1(y, hz1.at[y])
    each("y", lambda p: arrived(GY, "y", gy_v, p))

    def sum2(p, to):
        owner = y * nz + p
        acc = jnp.zeros(g2.shape[1:], F32)
        for j in range(ny):
            for k in range(nb):
                hit = jnp.where(ty_s[j, 0, k] == owner, 1.0, 0.0).astype(F32)
                acc = acc + hit * gy_v[j, k].astype(F32)
        to[...] = acc.astype(BF16)

    def send_sum2(p):
        sum2(p, h2.at[p])
        remote(HZ, "z", h2.at[p], hz2.at[z], p).start()

    each("z", send_sum2)
    sum2(z, hz2.at[z])

    each("t", lambda p: arrived(BASE, "t", ebuf, p))
    base = ebuf[0].astype(F32)
    for j in range(1, nt):
        base = base + ebuf[j].astype(F32)
    for k in range(nb):
        span = slice(k * BLOCK, (k + 1) * BLOCK)
        raised = tn_dot(low_t[:, span], up_at[k])
        out_ref[span, :] = (base[span] + ADAPTER_SCALE * raised).astype(BF16)

    each("y", lambda p: arrived(CNT, "y", all_ten, p))
    hits = jnp.where(all_ten[:, :, 0, :] == d, 1.0, 0.0).astype(F32)
    count = jnp.sum(hits) * BLOCK
    quota = jnp.full((8, 128), quo_s[d], jnp.int32).astype(F32)
    scale = (quota / jnp.maximum(jnp.full((8, 128), count, F32), 1.0))[:1, :1]
    each("y", lambda p: arrived(HY, "y", hz1, p))
    acc = hz1[0].astype(F32)
    for j in range(1, ny):
        acc = acc + hz1[j].astype(F32)
    da_ref[:, :first] = acc[:, :first] * scale
    db_ref[...] = acc[:, first:] * scale
    each("z", lambda p: arrived(HZ, "z", hz2, p))
    acc = hz2[0].astype(F32)
    for j in range(1, nz):
        acc = acc + hz2[j].astype(F32)
    da_ref[:, first:] = acc * scale

    def left(kind, line, src, dst_buf):
        each(line, lambda p: remote(kind, line, src(p), dst_buf.at[lines[line][0]], p).wait_send())

    left(TZ, "z", lambda p: tile, tz_v)
    left(TY, "y", lambda p: tile, ty_v)
    left(AZ, "z", lambda p: a1, row1)
    left(AY, "y", lambda p: a2, col2)
    left(WGT, "t", lambda p: w_hbm.at[pl.ds(p * feats, feats)], wbuf)
    left(VAL, "t", lambda p: vbuf.at[t], vbuf)
    left(SY, "y", lambda p: s1.at[p], r1)
    left(SZ, "z", lambda p: s2.at[p], r2)
    left(CNT, "y", lambda p: tz_v, all_ten)
    left(RANK, "t", lambda p: pbuf.at[t], pbuf)
    left(GZ, "z", lambda p: g1, gz_v)
    left(GY, "y", lambda p: g2, gy_v)
    left(BASE, "t", lambda p: bsend.at[p], ebuf)
    left(HY, "y", lambda p: h1.at[p], hz1)
    left(HZ, "z", lambda p: h2.at[p], hz2)
    gin_copy.wait()


def solution(mesh):
    nt = mesh.shape["tensor"]
    nz = LINE
    ny = mesh.shape["dp"] // nz

    def on_device(x, w, a, b, v, tenants, quotas):
        rows, feats = x.shape
        values = v.shape[1]
        _, rank, _ = b.shape
        nb = tenants.shape[0]
        first = feats // 2
        wide, half = first + values, feats - first
        most = max(nt, ny, nz)
        hbm = pl.BlockSpec(memory_space=pl.ANY)
        smem = pl.BlockSpec(memory_space=pltpu.SMEM)
        vmem = pl.BlockSpec(memory_space=pltpu.VMEM)
        out, gin, da, db = pl.pallas_call(
            functools.partial(kernel, nt, ny, nz),
            out_shape=(
                jax.ShapeDtypeStruct((rows, values), BF16),
                jax.ShapeDtypeStruct((rows, feats), BF16),
                jax.ShapeDtypeStruct((rank, feats), F32),
                jax.ShapeDtypeStruct((rank, values), F32),
            ),
            in_specs=[smem, smem, hbm, hbm, hbm, hbm, hbm],
            out_specs=(vmem, hbm, vmem, vmem),
            scratch_shapes=[
                pltpu.VMEM((8, 128), jnp.int32),
                pltpu.VMEM((nz, 8, 128), jnp.int32),
                pltpu.VMEM((ny, 8, 128), jnp.int32),
                pltpu.SMEM((nz, 8, 128), jnp.int32),
                pltpu.SMEM((ny, 8, 128), jnp.int32),
                pltpu.VMEM((ny, nz, 8, 128), jnp.int32),
                pltpu.VMEM((rows, feats), BF16),
                pltpu.VMEM((rank, wide), BF16),
                pltpu.VMEM((rank, half), BF16),
                pltpu.VMEM((nz, rank, wide), BF16),
                pltpu.VMEM((ny, rank, half), BF16),
                pltpu.VMEM((ny, nb, rank, wide), BF16),
                pltpu.VMEM((nz, nb, rank, half), BF16),
                pltpu.VMEM((ny, nb, rank, wide), BF16),
                pltpu.VMEM((nz, nb, rank, half), BF16),
                pltpu.VMEM((nt, rows, values), BF16),
                pltpu.VMEM((nt, feats, values), BF16),
                pltpu.VMEM((nt, 2 * rank, rows), BF16),
                pltpu.VMEM((nt, rows, values), BF16),
                pltpu.VMEM((nt, rows, values), BF16),
                pltpu.VMEM((nb, rank, wide), BF16),
                pltpu.VMEM((nb, rank, half), BF16),
                pltpu.VMEM((nz, nb, rank, wide), BF16),
                pltpu.VMEM((ny, nb, rank, half), BF16),
                pltpu.VMEM((ny, rank, wide), BF16),
                pltpu.VMEM((nz, rank, half), BF16),
                pltpu.VMEM((ny, rank, wide), BF16),
                pltpu.VMEM((nz, rank, half), BF16),
                pltpu.VMEM((rows, feats), BF16),
                pltpu.SemaphoreType.DMA((6,)),
                pltpu.SemaphoreType.DMA((15, most)),
                pltpu.SemaphoreType.DMA((15, most)),
            ],
            compiler_params=pltpu.CompilerParams(
                collective_id=0, has_side_effects=True, vmem_limit_bytes=32 << 20
            ),
        )(tenants, quotas, x, w, jnp.swapaxes(a[0], 0, 1), b[0], v)
        return out, gin, jnp.swapaxes(da, 0, 1)[None], db[None]

    return jax.shard_map(
        on_device,
        mesh=mesh,
        in_specs=(
            P("dp", "tensor"),
            P(None, "tensor"),
            P("dp", "tensor", None),
            P("dp", None, "tensor"),
            P("dp", "tensor"),
            P("dp"),
            P(),
        ),
        out_specs=(
            P("dp", "tensor"),
            P("dp", "tensor"),
            P("dp", "tensor", None),
            P("dp", None, "tensor"),
        ),
        check_vma=False,
    )
```

time: 250 us -> 76.9 us (0.31); the launches traced: 246 us -> 76.6 us
  waiting for transfers between devices: 76.1 us -> 0 us
  Pallas kernels: 0 us -> 67 us
  blocking collectives: 64.9 us -> 0 us
  starting transfers between devices: 33 us -> 0 us
  matrix products: 24.4 us -> 0 us
  local copies, waits for them, and re-layouts: 30.6 us -> 8.87 us
  between operations: 14.2 us -> 0.66 us
  other arithmetic: 3.02 us -> 0 us
    pallas_call x0 -> x1, Pallas kernels: none -> 67 us  [on_device(): pl.pallas_call(functools.partial(kernel, nt, ny, nz), out_shape=(jax.Shap...]
    all_gather x2 -> x0, waiting for transfers between devices: 40.3 us -> none  [the longest x1 25 us: on_device(): lax.all_gather(adapter_down_matrix, 'dp', axis=0, tiled=True)]
    all_gather x1 -> x0, blocking collectives: 39.9 us -> none  [on_device(): lax.all_gather(adapter_up_matrix, 'dp', axis=0, tiled=True)]
    all_to_all x4 -> x0, waiting for transfers between devices: 35.1 us -> none  [the longest x1 26.1 us: on_device(): lax.all_to_all(frozen_value_weight, 'tensor', split_axis=0, concat_axis=1...]
    all_to_all x4 -> x0, starting transfers between devices: 32.9 us -> none  [the longest x2 21.5 us: sent_to_all(): return lax.all_to_all(copies, axis, split_axis=0, concat_axis=0, tiled=True)]
    psum x1 -> x0, blocking collectives: 25 us -> none  [on_device(): lax.psum(low_part.astype(jnp.bfloat16), 'tensor').astype(jnp.float32)]
    dot_general x18 -> x0, matrix products: 24.4 us -> none  [the longest x1 12 us: on_device(): jnp.einsum('bo,bdr->odr', selector, pieces[0], precision=lax.Precision.HI...]
    slice x2 -> x0, local copies, waits for them, and re-layouts: 10.9 us -> none  [sent_together(): section = whole[..., at:at + column.shape[along]]]
  transfers between devices with their start and end apart: 6 -> 0, of which waited for: 5 -> 0; matrix products, arithmetic and copies ran while one was open for 8% -> 0% of each run, Pallas kernels for 0% -> 0%
where the time goes in v1:
time: 76.9 us; the launch traced here: 76.6 us
  Pallas kernels  67 us (87%)
  local copies, waits for them, and re-layouts  8.87 us (12%)
    pallas_call x1, Pallas kernels, on_device(): pl.pallas_call(functools.partial(kernel, nt, ny, nz), out_shape=(jax.Shap...  67 us
    unnamed x18, local copies, waits for them, and re-layouts  8.87 us

profile of v1, /device:TPU:1, one launch (start us, length us, event | category | flops | bytes accessed | tf_op | source)
XLA Modules:
  0.0 76.6 jit_solution(2575856894209184391)
XLA Ops:
  0.6 0.0 copy-start
  0.6 1.6 %copy-done = bf16[8192,128]{1,0:T(8,128)(2,1)S(1)} copy-done((bf16[8192,128]{1,0:T(8,128)(2,1)S(1)}, bf16[8192,128]{1,0:T(8,128)(2,1)}, u32[]{:S(2)}) %copy-start) | copy-done | bytes 2097176
  2.2 0.0 copy-start.1
  2.2 1.0 %copy-done.1 = bf16[256,1024]{1,0:T(8,128)(2,1)S(1)} copy-done((bf16[256,1024]{1,0:T(8,128)(2,1)S(1)}, bf16[256,1024]{1,0:T(8,128)(2,1)}, u32[]{:S(2)}) %copy-start.1) | copy-done | bytes 524312
  3.3 0.0 copy-start.2
  3.3 0.8 %copy-done.2 = bf16[256,128]{1,0:T(8,128)(2,1)S(1)} copy-done((bf16[256,128]{1,0:T(8,128)(2,1)S(1)}, bf16[256,128]{1,0:T(8,128)(2,1)}, u32[]{:S(2)}) %copy-start.2) | copy-done | bytes 65560
  4.1 0.0 copy-start.3
  4.1 0.8 copy-done.3
  4.9 0.0 copy-start.4
  4.9 0.7 copy-done.4
  5.6 0.0 copy-start.5
  5.6 0.7 copy-done.5
  6.2 0.0 copy-start.6
  6.2 0.7 copy-done.6
  6.9 67.0 %shard_map.102 = (bf16[256,128]{1,0:T(8,128)(2,1)S(1)}, bf16[256,1024]{1,0:T(8,128)(2,1)S(1)}, f32[16,1024]{1,0:T(8,128)S(1)}, f32[16,128]{1,0:T(8,128)S(1)}) custom-call(s32[2]{0:T(128)S(1)} %copy-done.5, s32[64]{0:T(128)S(1)} %copy-done.6, bf16[256,1024]{1,0:T(8,128)(2,1)S(1)} %copy-done.1, bf16[8192,128]{1,0:T(8,128)(2,1)S(1)} %copy-done, ...), custom_call_target="tpu_custom_call" | custom-call | tf_op jit(solution)/shard_map/pallas_call | solution.py:324
  73.9 0.6 copy.15
  74.5 0.8 %copy.16 = bf16[256,1024]{1,0:T(8,128)(2,1)} copy(bf16[256,1024]{1,0:T(8,128)(2,1)S(1)} %get-tuple-element.17) | data formatting | bytes 1048576
  75.3 0.6 copy.17
  76.0 0.6 copy.18
Async XLA Ops:
  0.6 1.6 %copy-start = (bf16[8192,128]{1,0:T(8,128)(2,1)S(1)}, bf16[8192,128]{1,0:T(8,128)(2,1)}, u32[]{:S(2)}) copy-start(bf16[8192,128]{1,0:T(8,128)(2,1)} %w_hbm.1) | copy-start | bytes 6291460
  2.2 1.0 %copy-start.1 = (bf16[256,1024]{1,0:T(8,128)(2,1)S(1)}, bf16[256,1024]{1,0:T(8,128)(2,1)}, u32[]{:S(2)}) copy-start(bf16[256,1024]{1,0:T(8,128)(2,1)} %x_hbm.1) | copy-start | bytes 1572868
  3.3 0.8 %copy-start.2 = (bf16[256,128]{1,0:T(8,128)(2,1)S(1)}, bf16[256,128]{1,0:T(8,128)(2,1)}, u32[]{:S(2)}) copy-start(bf16[256,128]{1,0:T(8,128)(2,1)} %v_hbm.1) | copy-start | bytes 196612
  4.1 0.8 copy-start.3
  4.9 0.7 copy-start.4
  5.6 0.7 copy-start.5
  6.2 0.7 copy-start.6

commit v2 on v1

--- a/solution.py
+++ b/solution.py
@@ -14,7 +14,7 @@
 BF16 = jnp.bfloat16
 F32 = jnp.float32
 
-TZ, TY, AZ, AY, SY, SZ, VAL, WGT, RANK, BASE, GZ, GY, HY, HZ, CNT = range(15)
+TZ, TY, AZ, AY, SY, SZ, VAL, FWD, WGT, RANK, PRE, BASE, GZ, GY, HY, HZ, CNT = range(17)
 
 
 def far_first(n):
@@ -31,16 +31,19 @@
 
 def kernel(
     nt, ny, nz,
-    ten_s, quo_s, x_hbm, w_hbm, a_hbm, b_hbm, v_hbm,
-    out_ref, gin_hbm, da_ref, db_ref,
-    tile, tz_v, ty_v, tz_s, ty_s, all_ten,
+    ten_hbm, quo_hbm, x_hbm, w_hbm, a_hbm, b_hbm, v_hbm,
+    out_ref, gin_v, da_ref, db_ref,
+    ten_s, quo_s, tile, tz_v, ty_v, tz_s, ty_s, all_ten,
     xv, a1, a2, row1, col2, s1, s2, r1, r2,
-    vbuf, wbuf, pbuf, bsend, ebuf, g1, g2, gz_v, gy_v, h1, h2, hz1, hz2, gin_v,
+    vbuf, wbuf, pbuf, presend, prebuf, keep, bsend, ebuf, g1, g2, gz_v, gy_v, h1, h2, hz1, hz2,
     loc, ss, rs,
 ):
     t = lax.axis_index("tensor")
     d = lax.axis_index("dp")
     y, z = lax.div(d, nz), lax.rem(d, nz)
+    nx = nt // 2
+    x, core = lax.div(t, 2), lax.rem(t, 2)
+    twin = t + 1 - 2 * core
     rows, feats = xv.shape
     nb = rows // BLOCK
     half = a2.shape[1]
@@ -82,16 +85,24 @@
 
         lax.fori_loop(1, n, body, 0)
 
+    barrier = pltpu.get_barrier_semaphore()
+    for line in ("t", "y", "z"):
+        dev = lines[line][2]
+        each(line, lambda p: pl.semaphore_signal(barrier, inc=1, device_id=dev(p), device_id_type=MESH))
     local = [
         pltpu.make_async_copy(a_hbm.at[:, pl.ds(0, first)], a1.at[:, pl.ds(0, first)], loc.at[0]),
         pltpu.make_async_copy(b_hbm, a1.at[:, pl.ds(first, values)], loc.at[1]),
         pltpu.make_async_copy(a_hbm.at[:, pl.ds(first, half)], a2, loc.at[2]),
+        pltpu.make_async_copy(ten_hbm, ten_s, loc.at[6]),
+        pltpu.make_async_copy(v_hbm, vbuf.at[t], loc.at[4]),
         pltpu.make_async_copy(x_hbm, xv, loc.at[3]),
-        pltpu.make_async_copy(v_hbm, vbuf.at[t], loc.at[4]),
         pltpu.make_async_copy(w_hbm.at[pl.ds(t * feats, feats)], wbuf.at[t], loc.at[5]),
+        pltpu.make_async_copy(quo_hbm, quo_s, loc.at[7]),
     ]
     for copy in local:
         copy.start()
+    get_a, get_b, get_a2, get_ten, get_v, get_x, get_w, get_quo = local
+    get_ten.wait()
     lane = lax.broadcasted_iota(jnp.int32, tile.shape, 1)
     mine = jnp.full(tile.shape, -1, jnp.int32)
     for k in range(nb):
@@ -99,25 +110,38 @@
     tile[...] = mine
     tz_v[z] = mine
     ty_v[y] = mine
-
-    barrier = pltpu.get_barrier_semaphore()
-    for line in ("t", "y", "z"):
-        dev = lines[line][2]
-        each(line, lambda p: pl.semaphore_signal(barrier, inc=1, device_id=dev(p), device_id_type=MESH))
-    local[0].wait()
-    local[1].wait()
-    local[2].wait()
+    get_a.wait()
+    get_b.wait()
+    get_a2.wait()
     row1[z] = a1[...]
     col2[y] = a2[...]
+    get_v.wait()
     pl.semaphore_wait(barrier, nt + ny + nz - 3)
 
     peers("z", lambda p: remote(TZ, "z", tile, tz_v.at[z], p).start())
     peers("y", lambda p: remote(TY, "y", tile, ty_v.at[y], p).start())
     peers("z", lambda p: remote(AZ, "z", a1, row1.at[z], p).start())
     peers("y", lambda p: remote(AY, "y", a2, col2.at[y], p).start())
-    peers("t", lambda p: remote(WGT, "t", w_hbm.at[pl.ds(p * feats, feats)], wbuf.at[t], p).start())
-    local[4].wait()
-    peers("t", lambda p: remote(VAL, "t", vbuf.at[t], vbuf.at[t], p).start())
+
+    near = [off for off in range(1, nx) if min(off, nx - off) == 1]
+    far = [off for off in range(1, nx) if off not in near]
+
+    def chip(off):
+        return lax.rem(x + off, nx)
+
+    def value_to(p):
+        return remote(VAL, "t", vbuf.at[t], vbuf.at[t], p)
+
+    def weight_to(p):
+        return remote(WGT, "t", w_hbm.at[pl.ds(p * feats, feats)], wbuf.at[t], p)
+
+    for off in far + near:
+        value_to(2 * chip(off) + core).start()
+    value_to(twin).start()
+    weight_to(twin).start()
+    for off in near:
+        weight_to(2 * chip(off) + core).start()
+        weight_to(2 * chip(off) + 1 - core).start()
 
     each("z", lambda p: arrived(TZ, "z", tz_v, p))
     each("y", lambda p: arrived(TY, "y", ty_v, p))
@@ -154,8 +178,56 @@
     pick2(z, r2.at[z])
     peers("y", lambda p: remote(CNT, "y", tz_v, all_ten.at[y], p).start())
 
-    local[3].wait()
-    local[5].wait()
+    def forward(p):
+        return pltpu.make_async_remote_copy(
+            src_ref=vbuf.at[p], dst_ref=vbuf.at[p], send_sem=ss.at[FWD, p], recv_sem=rs.at[VAL, p],
+            device_id={"tensor": twin}, device_id_type=MESH,
+        )
+
+    for off in far + near:
+        p = 2 * chip(off) + core
+        arrived(VAL, "t", vbuf, p)
+        forward(p).start()
+
+    def base_of(p):
+        return jnp.dot(xv[...], wbuf[p], preferred_element_type=F32)
+
+    def pre_to(q):
+        return pltpu.make_async_remote_copy(
+            src_ref=presend.at[q], dst_ref=prebuf.at[q], send_sem=ss.at[PRE, q], recv_sem=rs.at[PRE, q],
+            device_id={"tensor": twin}, device_id_type=MESH,
+        )
+
+    def halves(q):
+        presend[q] = base_of(2 * q + 1 - core).astype(BF16)
+        pre_to(q).start()
+        keep[q] = base_of(2 * q + core)
+
+    def both(q):
+        pre_to(q).wait_recv()
+        return keep[q] + prebuf[q].astype(F32)
+
+    def base_to(q):
+        return pltpu.make_async_remote_copy(
+            src_ref=bsend.at[q], dst_ref=ebuf.at[x], send_sem=ss.at[BASE, q], recv_sem=rs.at[BASE, x],
+            device_id={"tensor": 2 * q + core}, device_id_type=MESH,
+        )
+
+    def base_from(q):
+        pltpu.make_async_remote_copy(
+            src_ref=bsend.at[q], dst_ref=ebuf.at[q], send_sem=ss.at[BASE, q], recv_sem=rs.at[BASE, q],
+            device_id={"tensor": 2 * q + core}, device_id_type=MESH,
+        ).wait_recv()
+
+    def send_base(q):
+        bsend[q] = both(q).astype(BF16)
+        base_to(q).start()
+
+    get_x.wait()
+    get_w.wait()
+    arrived(WGT, "t", wbuf, twin)
+    halves(x)
+
     each("y", lambda p: arrived(SY, "y", r1, p))
     each("z", lambda p: arrived(SZ, "z", r2, p))
 
@@ -174,6 +246,13 @@
         pbuf[t, :rank, span] = low.astype(BF16)
         pbuf[t, rank:, span] = grad.astype(BF16)
     peers("t", lambda p: remote(RANK, "t", pbuf.at[t], pbuf.at[t], p).start())
+    for off in far:
+        weight_to(2 * chip(off) + core).start()
+        weight_to(2 * chip(off) + 1 - core).start()
+    for off in near:
+        arrived(WGT, "t", wbuf, 2 * chip(off) + core)
+        arrived(WGT, "t", wbuf, 2 * chip(off) + 1 - core)
+        halves(chip(off))
     each("t", lambda p: arrived(RANK, "t", pbuf, p))
     total = pbuf[0].astype(F32)
     for j in range(1, nt):
@@ -193,19 +272,69 @@
     gz_v[z] = g1[...]
     gy_v[y] = g2[...]
 
-    def base_of(p):
-        return jnp.dot(xv[...], wbuf[p], preferred_element_type=F32).astype(BF16)
-
-    ebuf[t] = base_of(t)
-
-    def send_base(p):
-        arrived(WGT, "t", wbuf, p)
-        bsend[p] = base_of(p)
-        remote(BASE, "t", bsend.at[p], ebuf.at[t], p).start()
-
-    each("t", send_base)
-
-    each("t", lambda p: arrived(VAL, "t", vbuf, p))
+    def left(kind, line, src, dst_buf):
+        each(line, lambda p: remote(kind, line, src(p), dst_buf.at[lines[line][0]], p).wait_send())
+
+    for off in near:
+        send_base(chip(off))
+    left(TZ, "z", lambda p: tile, tz_v)
+    left(TY, "y", lambda p: tile, ty_v)
+    left(AZ, "z", lambda p: a1, row1)
+    left(AY, "y", lambda p: a2, col2)
+    left(SY, "y", lambda p: s1.at[p], r1)
+    left(SZ, "z", lambda p: s2.at[p], r2)
+    left(CNT, "y", lambda p: tz_v, all_ten)
+    left(RANK, "t", lambda p: pbuf.at[t], pbuf)
+    for off in far + near:
+        value_to(2 * chip(off) + core).wait_send()
+        forward(2 * chip(off) + core).wait_send()
+    value_to(twin).wait_send()
+
+    for off in far:
+        arrived(WGT, "t", wbuf, 2 * chip(off) + core)
+        arrived(WGT, "t", wbuf, 2 * chip(off) + 1 - core)
+        halves(chip(off))
+
+    each("z", lambda p: arrived(GZ, "z", gz_v, p))
+
+    def sum1(p, to):
+        owner = p * nz + z
+        acc = jnp.zeros(g1.shape[1:], F32)
+        for j in range(nz):
+            for k in range(nb):
+                hit = jnp.where(tz_s[j, 0, k] == owner, 1.0, 0.0).astype(F32)
+                acc = acc + hit * gz_v[j, k].astype(F32)
+        to[...] = acc.astype(BF16)
+
+    def send_sum1(p):
+        sum1(p, h1.at[p])
+        remote(HY, "y", h1.at[p], hz1.at[y], p).start()
+
+    each("y", send_sum1)
+    for off in far:
+        send_base(chip(off))
+    sum1(y, hz1.at[y])
+    each("y", lambda p: arrived(GY, "y", gy_v, p))
+
+    def sum2(p, to):
+        owner = y * nz + p
+        acc = jnp.zeros(g2.shape[1:], F32)
+        for j in range(ny):
+            for k in range(nb):
+                hit = jnp.where(ty_s[j, 0, k] == owner, 1.0, 0.0).astype(F32)
+                acc = acc + hit * gy_v[j, k].astype(F32)
+        to[...] = acc.astype(BF16)
+
+    def send_sum2(p):
+        sum2(p, h2.at[p])
+        remote(HZ, "z", h2.at[p], hz2.at[z], p).start()
+
+    each("z", send_sum2)
+    sum2(z, hz2.at[z])
+
+    arrived(VAL, "t", vbuf, twin)
+    for off in far + near:
+        arrived(VAL, "t", vbuf, 2 * chip(off) + 1 - core)
     tiles = 4
     width = feats // tiles
     for i in range(tiles):
@@ -220,54 +349,18 @@
             else:
                 at = second_at[k][:, i * width - first : (i + 1) * width - first]
             gin_v[span, cols] = (acc[span] + tn_dot(grad_t[:, span], at)).astype(BF16)
-    gin_copy = pltpu.make_async_copy(gin_v, gin_hbm, loc.at[2])
-    gin_copy.start()
-
-    each("z", lambda p: arrived(GZ, "z", gz_v, p))
-
-    def sum1(p, to):
-        owner = p * nz + z
-        acc = jnp.zeros(g1.shape[1:], F32)
-        for j in range(nz):
-            for k in range(nb):
-                hit = jnp.where(tz_s[j, 0, k] == owner, 1.0, 0.0).astype(F32)
-                acc = acc + hit * gz_v[j, k].astype(F32)
-        to[...] = acc.astype(BF16)
-
-    def send_sum1(p):
-        sum1(p, h1.at[p])
-        remote(HY, "y", h1.at[p], hz1.at[y], p).start()
-
-    each("y", send_sum1)
-    sum1(y, hz1.at[y])
-    each("y", lambda p: arrived(GY, "y", gy_v, p))
-
-    def sum2(p, to):
-        owner = y * nz + p
-        acc = jnp.zeros(g2.shape[1:], F32)
-        for j in range(ny):
-            for k in range(nb):
-                hit = jnp.where(ty_s[j, 0, k] == owner, 1.0, 0.0).astype(F32)
-                acc = acc + hit * gy_v[j, k].astype(F32)
-        to[...] = acc.astype(BF16)
-
-    def send_sum2(p):
-        sum2(p, h2.at[p])
-        remote(HZ, "z", h2.at[p], hz2.at[z], p).start()
-
-    each("z", send_sum2)
-    sum2(z, hz2.at[z])
-
-    each("t", lambda p: arrived(BASE, "t", ebuf, p))
-    base = ebuf[0].astype(F32)
-    for j in range(1, nt):
-        base = base + ebuf[j].astype(F32)
+
+    base = both(x)
+    for off in near + far:
+        base_from(chip(off))
+        base = base + ebuf[chip(off)].astype(F32)
     for k in range(nb):
         span = slice(k * BLOCK, (k + 1) * BLOCK)
         raised = tn_dot(low_t[:, span], up_at[k])
         out_ref[span, :] = (base[span] + ADAPTER_SCALE * raised).astype(BF16)
 
     each("y", lambda p: arrived(CNT, "y", all_ten, p))
+    get_quo.wait()
     hits = jnp.where(all_ten[:, :, 0, :] == d, 1.0, 0.0).astype(F32)
     count = jnp.sum(hits) * BLOCK
     quota = jnp.full((8, 128), quo_s[d], jnp.int32).astype(F32)
@@ -284,25 +377,26 @@
         acc = acc + hz2[j].astype(F32)
     da_ref[:, first:] = acc * scale
 
-    def left(kind, line, src, dst_buf):
-        each(line, lambda p: remote(kind, line, src(p), dst_buf.at[lines[line][0]], p).wait_send())
-
-    left(TZ, "z", lambda p: tile, tz_v)
-    left(TY, "y", lambda p: tile, ty_v)
-    left(AZ, "z", lambda p: a1, row1)
-    left(AY, "y", lambda p: a2, col2)
-    left(WGT, "t", lambda p: w_hbm.at[pl.ds(p * feats, feats)], wbuf)
-    left(VAL, "t", lambda p: vbuf.at[t], vbuf)
-    left(SY, "y", lambda p: s1.at[p], r1)
-    left(SZ, "z", lambda p: s2.at[p], r2)
-    left(CNT, "y", lambda p: tz_v, all_ten)
-    left(RANK, "t", lambda p: pbuf.at[t], pbuf)
+    weight_to(twin).wait_send()
+    for off in far + near:
+        weight_to(2 * chip(off) + core).wait_send()
+        weight_to(2 * chip(off) + 1 - core).wait_send()
+        base_to(chip(off)).wait_send()
+        pre_to(chip(off)).wait_send()
+    pre_to(x).wait_send()
     left(GZ, "z", lambda p: g1, gz_v)
     left(GY, "y", lambda p: g2, gy_v)
-    left(BASE, "t", lambda p: bsend.at[p], ebuf)
     left(HY, "y", lambda p: h1.at[p], hz1)
     left(HZ, "z", lambda p: h2.at[p], hz2)
-    gin_copy.wait()
+
+
+def write_out(out_v, gin_v, da_v, db_v, out_hbm, gin_hbm, da_hbm, db_hbm, sems):
+    pairs = ((gin_v, gin_hbm), (out_v, out_hbm), (da_v, da_hbm), (db_v, db_hbm))
+    copies = [pltpu.make_async_copy(a, b, sems.at[i]) for i, (a, b) in enumerate(pairs)]
+    for copy in copies:
+        copy.start()
+    for copy in copies:
+        copy.wait()
 
 
 def solution(mesh):
@@ -318,8 +412,8 @@
         first = feats // 2
         wide, half = first + values, feats - first
         most = max(nt, ny, nz)
-        hbm = pl.BlockSpec(memory_space=pl.ANY)
-        smem = pl.BlockSpec(memory_space=pltpu.SMEM)
+        hbm = pl.BlockSpec(memory_space=pltpu.MemorySpace.HBM)
+        anywhere = pl.BlockSpec(memory_space=pl.ANY)
         vmem = pl.BlockSpec(memory_space=pltpu.VMEM)
         out, gin, da, db = pl.pallas_call(
             functools.partial(kernel, nt, ny, nz),
@@ -329,9 +423,11 @@
                 jax.ShapeDtypeStruct((rank, feats), F32),
                 jax.ShapeDtypeStruct((rank, values), F32),
             ),
-            in_specs=[smem, smem, hbm, hbm, hbm, hbm, hbm],
-            out_specs=(vmem, hbm, vmem, vmem),
+            in_specs=[hbm] * 7,
+            out_specs=(vmem,) * 4,
             scratch_shapes=[
+                pltpu.SMEM((nb,), jnp.int32),
+                pltpu.SMEM(quotas.shape, jnp.int32),
                 pltpu.VMEM((8, 128), jnp.int32),
                 pltpu.VMEM((nz, 8, 128), jnp.int32),
                 pltpu.VMEM((ny, 8, 128), jnp.int32),
@@ -350,8 +446,11 @@
                 pltpu.VMEM((nt, rows, values), BF16),
                 pltpu.VMEM((nt, feats, values), BF16),
                 pltpu.VMEM((nt, 2 * rank, rows), BF16),
-                pltpu.VMEM((nt, rows, values), BF16),
-                pltpu.VMEM((nt, rows, values), BF16),
+                pltpu.VMEM((nt // 2, rows, values), BF16),
+                pltpu.VMEM((nt // 2, rows, values), BF16),
+                pltpu.VMEM((nt // 2, rows, values), F32),
+                pltpu.VMEM((nt // 2, rows, values), BF16),
+                pltpu.VMEM((nt // 2, rows, values), BF16),
                 pltpu.VMEM((nb, rank, wide), BF16),
                 pltpu.VMEM((nb, rank, half), BF16),
                 pltpu.VMEM((nz, nb, rank, wide), BF16),
@@ -360,15 +459,30 @@
                 pltpu.VMEM((nz, rank, half), BF16),
                 pltpu.VMEM((ny, rank, wide), BF16),
                 pltpu.VMEM((nz, rank, half), BF16),
-                pltpu.VMEM((rows, feats), BF16),
-                pltpu.SemaphoreType.DMA((6,)),
-                pltpu.SemaphoreType.DMA((15, most)),
-                pltpu.SemaphoreType.DMA((15, most)),
+                pltpu.SemaphoreType.DMA((8,)),
+                pltpu.SemaphoreType.DMA((17, most)),
+                pltpu.SemaphoreType.DMA((17, most)),
             ],
             compiler_params=pltpu.CompilerParams(
-                collective_id=0, has_side_effects=True, vmem_limit_bytes=32 << 20
+                collective_id=0, has_side_effects=True, vmem_limit_bytes=48 << 20
             ),
-        )(tenants, quotas, x, w, jnp.swapaxes(a[0], 0, 1), b[0], v)
+        )(*[
+            pltpu.with_memory_space_constraint(arg, pltpu.MemorySpace.HBM)
+            for arg in (tenants, quotas, x, w, jnp.swapaxes(a[0], 0, 1), b[0], v)
+        ])
+        out, gin, da, db = pl.pallas_call(
+            write_out,
+            out_shape=(
+                jax.ShapeDtypeStruct((rows, values), BF16),
+                jax.ShapeDtypeStruct((rows, feats), BF16),
+                jax.ShapeDtypeStruct((rank, feats), F32),
+                jax.ShapeDtypeStruct((rank, values), F32),
+            ),
+            in_specs=[anywhere] * 4,
+            out_specs=(hbm,) * 4,
+            scratch_shapes=[pltpu.SemaphoreType.DMA((4,))],
+            compiler_params=pltpu.CompilerParams(vmem_limit_bytes=4 << 20),
+        )(out, gin, da, db)
         return out, gin, jnp.swapaxes(da, 0, 1)[None], db[None]
 
     return jax.shard_map(

time: 76.9 us -> 58.8 us (0.76)
  Pallas kernels: 67 us -> 57.1 us
  local copies, waits for them, and re-layouts: 8.87 us -> 0 us
    pallas_call x1, Pallas kernels: 67 us -> 56.2 us  [on_device(): pl.pallas_call(functools.partial(kernel, nt, ny, nz), out_shape=(jax.Shap...]
    unnamed x18 -> x0, local copies, waits for them, and re-layouts: 8.87 us -> none
    pallas_call x0 -> x1, Pallas kernels: none -> 0.86 us  [on_device(): pl.pallas_call(write_out, out_shape=(jax.ShapeDtypeStruct((rows, values),...]
where the time goes in v2:
time: 58.8 us; the launch traced here: 57.7 us
  Pallas kernels  57.1 us (97%)
  between operations  0.64 us (1%)
    pallas_call x1, Pallas kernels, on_device(): pl.pallas_call(functools.partial(kernel, nt, ny, nz), out_shape=(jax.Shap...  56.2 us

profile of v2, /device:TPU:1, one launch (start us, length us, event | category | flops | bytes accessed | tf_op | source)
XLA Modules:
  0.0 57.7 jit_solution(5891715313769884821)
XLA Ops:
  0.6 56.2 %shard_map.102 = (bf16[256,128]{1,0:T(8,128)(2,1)S(1)}, bf16[256,1024]{1,0:T(8,128)(2,1)S(1)}, f32[16,1024]{1,0:T(8,128)S(1)}, f32[16,128]{1,0:T(8,128)S(1)}) custom-call(s32[2]{0:T(128)} %ten_hbm.1, s32[64]{0:T(128)} %quo_hbm.1, bf16[256,1024]{1,0:T(8,128)(2,1)} %x_hbm.1, bf16[8192,128]{1,0:T(8,128)(2,1)} %w_hbm.1, bf16[16,1024]{1,0:T(8,128)(2,1)} %bitcast.8, ...), custom_call_target="tpu_custom_call" | custom-call | tf_op jit(solution)/shard_map/pallas_call | solution.py:418
  56.9 0.9 %shard_map.103 = (bf16[256,128]{1,0:T(8,128)(2,1)}, bf16[256,1024]{1,0:T(8,128)(2,1)}, f32[16,1024]{1,0:T(8,128)}, f32[16,128]{1,0:T(8,128)}) custom-call(bf16[256,128]{1,0:T(8,128)(2,1)S(1)} %get-tuple-element.12.out_v, bf16[256,1024]{1,0:T(8,128)(2,1)S(1)} %get-tuple-element.13.gin_v, f32[16,1024]{1,0:T(8,128)S(1)} %get-tuple-element.14.da_v, ...), custom_call_target="tpu_custom_call" | custom-call | tf_op jit(solution)/shard_map/pallas_call | solution.py:473

commit v3 on v2

v3 whole, which is shorter than its diff:
```python
import functools

import jax
import jax.numpy as jnp
from jax import lax
from jax.experimental import pallas as pl
from jax.experimental.pallas import tpu as pltpu
from jax.sharding import PartitionSpec as P

MESH = pl.DeviceIdType.MESH
BLOCK = 128
LINE = 8
ADAPTER_SCALE = 2.0
BF16 = jnp.bfloat16
F32 = jnp.float32

TZ, TY, AZ, AY, VAL, FWD, BASE, HY, HZ, CNT, SY, SZ, RANK, GZ, GY, WGT, PRE, SHARE, SY2, SZ2 = range(20)
SECOND = 10
KINDS = SECOND + GY + 1


def far_first(n):
    return sorted(range(1, n), key=lambda off: (-min(off, n - off), off))


def nt_dot(a, b):
    return lax.dot_general(a, b, (((1,), (1,)), ((), ())), preferred_element_type=F32)


def tn_dot(a, b):
    return lax.dot_general(a, b, (((0,), (0,)), ((), ())), preferred_element_type=F32)


def kernel(
    nt, ny, nz,
    ten_hbm, quo_hbm, x_hbm, w_hbm, a_hbm, b_hbm, v_hbm,
    out_hbm, gin_hbm, da_hbm, db_hbm,
    out_v, gin_v, da_v, db_v, ten_s, quo_s, tile, tz_v, ty_v, tz_s, ty_s, all_ten,
    xv, row1, col2, s1, s2, r1_first, r1_second, r2_first, r2_second,
    vbuf, wbuf, pbuf, presend, prebuf, keep, bsend, ebuf, g1, g2, gz_v, gy_v, acc1, acc2, h1, h2, hz1, hz2, gin_acc,
    loc, ss, rs, wgt_rs, pre_rs,
):
    t = lax.axis_index("tensor")
    d = lax.axis_index("dp")
    y, z = lax.div(d, nz), lax.rem(d, nz)
    nx = nt // 2
    x, core = lax.div(t, 2), lax.rem(t, 2)
    twin = t + 1 - 2 * core
    rows, feats = xv.shape
    nb = rows // BLOCK
    rank, half = col2.shape[1:]
    r1, r2 = (r1_first, r1_second), (r2_first, r2_second)
    first = feats - half
    values = v_hbm.shape[1]

    lines = {
        "t": (t, nt, lambda p: {"tensor": p}),
        "y": (y, ny, lambda p: {"dp": p * nz + z}),
        "z": (z, nz, lambda p: {"dp": y * nz + p}),
    }

    def remote(kind, line, src, dst, peer, recv=None):
        return pltpu.make_async_remote_copy(
            src_ref=src, dst_ref=dst, send_sem=ss.at[kind], recv_sem=rs.at[kind] if recv is None else recv,
            device_id=lines[line][2](peer), device_id_type=MESH,
        )

    def all_of(line, buf, recv, send=0):
        me, n, dev = lines[line]
        return pltpu.make_async_remote_copy(
            src_ref=buf, dst_ref=buf, send_sem=ss.at[send], recv_sem=recv,
            device_id=dev(lax.rem(me + 1, n)), device_id_type=MESH,
        )

    def arrived(kind, line, buf):
        others = lines[line][1] - 1
        if others:
            all_of(line, buf.at[pl.ds(0, others)], rs.at[kind]).wait_recv()

    def left(kind, line, buf, copies=None):
        others = lines[line][1] - 1 if copies is None else copies
        if others:
            all_of(line, buf.at[pl.ds(0, others)], rs.at[0], kind).wait_send()

    def left_both(kind, line, buf):
        others = lines[line][1] - 1
        if others:
            all_of(line, buf.at[:, pl.ds(0, others)], rs.at[0], kind).wait_send()

    def peers(line, fn):
        me, n, _ = lines[line]
        for off in far_first(n):
            fn(lax.rem(me + off, n))

    def each(line, fn):
        me, n, _ = lines[line]

        def body(off, carry):
            fn(lax.rem(me + off, n))
            return carry

        lax.fori_loop(1, n, body, 0)

    barrier = pltpu.get_barrier_semaphore()
    for line in ("t", "y", "z"):
        dev = lines[line][2]
        each(line, lambda p: pl.semaphore_signal(barrier, inc=1, device_id=dev(p), device_id_type=MESH))
    local = [
        pltpu.make_async_copy(ten_hbm, ten_s, loc.at[0]),
        pltpu.make_async_copy(a_hbm.at[:, pl.ds(0, first)], row1.at[z, :, pl.ds(0, first)], loc.at[1]),
        pltpu.make_async_copy(b_hbm, row1.at[z, :, pl.ds(first, values)], loc.at[2]),
        pltpu.make_async_copy(a_hbm.at[:, pl.ds(first, half)], col2.at[y], loc.at[3]),
        pltpu.make_async_copy(x_hbm, xv, loc.at[4]),
        pltpu.make_async_copy(v_hbm, vbuf.at[t], loc.at[5]),
        pltpu.make_async_copy(w_hbm.at[pl.ds(t * feats, feats)], wbuf.at[t], loc.at[6]),
        pltpu.make_async_copy(quo_hbm, quo_s, loc.at[7]),
    ]
    for copy in local:
        copy.start()
    local[0].wait()
    lane = lax.broadcasted_iota(jnp.int32, tile.shape, 1)
    mine = jnp.full(tile.shape, -1, jnp.int32)
    for k in range(nb):
        mine = jnp.where(lane == k, ten_s[k], mine)
    tile[...] = mine
    tz_v[z] = mine
    ty_v[y] = mine
    pl.semaphore_wait(barrier, nt + ny + nz - 3)

    def adapter_to_z(p):
        remote(AZ, "z", a_hbm.at[:, pl.ds(0, first)], row1.at[z, :, pl.ds(0, first)], p).start()
        remote(AZ, "z", b_hbm, row1.at[z, :, pl.ds(first, values)], p).start()

    peers("z", lambda p: remote(TZ, "z", tile, tz_v.at[z], p).start())
    peers("y", lambda p: remote(TY, "y", tile, ty_v.at[y], p).start())
    peers("z", adapter_to_z)
    peers("y", lambda p: remote(AY, "y", a_hbm.at[:, pl.ds(first, half)], col2.at[y], p).start())

    near = [off for off in range(1, nx) if min(off, nx - off) == 1]
    far = [off for off in range(1, nx) if off not in near]

    def chip(off):
        return lax.rem(x + off, nx)

    def value_to(p):
        return remote(VAL, "t", vbuf.at[t], vbuf.at[t], p)

    def weight_to(p, part=0, parts=1):
        size = feats // parts
        return remote(
            WGT, "t", w_hbm.at[pl.ds(p * feats + part * size, size)],
            wbuf.at[t, pl.ds(part * size, size)], p, wgt_rs.at[t],
        )

    def weight_arrived(p):
        all_of("t", wbuf.at[p], wgt_rs.at[p]).wait_recv()

    def pair(offs):
        return [2 * chip(off) + c for off in offs for c in (core, 1 - core)]

    ways = [(line, step) for line in ("y", "z") for step in (1, -1) if lines[line][1] > 1]
    mine_half = lax.rem(y + z, 2)
    rows_half = feats // 2
    rows_share = rows_half // len(ways)

    def share(p, i):
        line, step = ways[i]
        me, n, _ = lines[line]
        span = pl.ds(mine_half * rows_half + i * rows_share, rows_share)
        return remote(SHARE, line, wbuf.at[p, span], wbuf.at[p, span], lax.rem(me + step + n, n))

    near_weights = pair(near)
    shared = (pair(far), near_weights[::2])
    count_shared = len(shared[0]) + len(shared[1])
    weight_to(twin).start()
    for p in shared[0] + shared[1]:
        weight_to(p, mine_half, 2).start()
    for p in near_weights[1::2]:
        weight_to(p, 0, 4).start()

    arrived(TZ, "z", tz_v)
    arrived(TY, "y", ty_v)
    to_z = pltpu.make_async_copy(tz_v, tz_s, loc.at[0])
    to_y = pltpu.make_async_copy(ty_v, ty_s, loc.at[1])
    to_z.start()
    to_y.start()
    all_ten[y] = tz_v[...]
    to_z.wait()
    to_y.wait()
    for copy in local[1:4]:
        copy.wait()

    def pick1(k, p):
        return row1[lax.rem(ty_s[p, 0, k], nz)]

    def pick2(k, p):
        return col2[lax.div(tz_s[p, 0, k], nz)]

    def send1(k, p):
        s1[k, p] = pick1(k, p)
        kind, recv = (SY if k == 0 else SY2), rs.at[SY + k * SECOND]
        remote(kind, "y", s1.at[k, p], r1[k].at[y], p, recv).start()

    def send2(k, p):
        s2[k, p] = pick2(k, p)
        kind, recv = (SZ if k == 0 else SZ2), rs.at[SZ + k * SECOND]
        remote(kind, "z", s2.at[k, p], r2[k].at[z], p, recv).start()

    arrived(AZ, "z", row1)
    peers("y", lambda p: send1(0, p))
    arrived(AY, "y", col2)
    peers("z", lambda p: send2(0, p))
    for k in range(nb):
        r1[k][y] = pick1(k, y)
        r2[k][z] = pick2(k, z)

    def base_of(p):
        return jnp.dot(xv[...], wbuf[p], preferred_element_type=F32)

    def pre_to(q):
        return pltpu.make_async_remote_copy(
            src_ref=presend.at[q], dst_ref=prebuf.at[q], send_sem=ss.at[PRE], recv_sem=pre_rs.at[q],
            device_id={"tensor": twin}, device_id_type=MESH,
        )

    def halves(q):
        presend[q] = base_of(2 * q + 1 - core).astype(BF16)
        pre_to(q).start()
        keep[q] = base_of(2 * q + core)

    def both(q):
        pre_to(q).wait_recv()
        return keep[q] + prebuf[q].astype(F32)

    def base_to(q):
        return pltpu.make_async_remote_copy(
            src_ref=bsend.at[q], dst_ref=ebuf.at[x], send_sem=ss.at[BASE], recv_sem=rs.at[BASE],
            device_id={"tensor": 2 * q + core}, device_id_type=MESH,
        )

    def send_base(q):
        bsend[q] = both(q).astype(BF16)
        base_to(q).start()

    def forward(p):
        return pltpu.make_async_remote_copy(
            src_ref=vbuf.at[p], dst_ref=vbuf.at[p], send_sem=ss.at[FWD], recv_sem=rs.at[FWD],
            device_id={"tensor": twin}, device_id_type=MESH,
        )

    local[4].wait()
    local[5].wait()
    local[6].wait()
    weight_arrived(twin)
    halves(x)
    left(SY, "y", s1.at[0])
    left(SZ, "z", s2.at[0])

    def send_rest():
        for k in range(1, nb):
            peers("y", lambda p: send1(k, p))
            peers("z", lambda p: send2(k, p))

    pl.when(core == 0)(send_rest)
    for group in shared:
        for p in group:
            all_of("t", wbuf.at[p, pl.ds(0, rows_half)], wgt_rs.at[p]).wait_recv()
        if group is shared[0]:
            pl.when(core == 1)(send_rest)
        for i in range(len(ways)):
            for p in group:
                share(p, i).start()
    peers("y", lambda p: remote(CNT, "y", tz_v, all_ten.at[y], p).start())

    first_at, second_at, up_at = [], [], []

    def rank_products(k):
        arrived(SY + k * SECOND, "y", r1[k])
        arrived(SZ + k * SECOND, "z", r2[k])
        tenant = ten_s[k]
        part1 = r1[k][lax.div(tenant, nz)]
        at2 = r2[k][lax.rem(tenant, nz)]
        at1, up = part1[:, :first], part1[:, first:]
        first_at.append(at1)
        second_at.append(at2)
        up_at.append(up)
        span = pl.ds(k * BLOCK, BLOCK)
        low = nt_dot(at1, xv[span, :first]) + nt_dot(at2, xv[span, first:])
        grad = ADAPTER_SCALE * nt_dot(up, vbuf[t, span, :])
        pbuf[k, t, :rank] = low.astype(BF16)
        pbuf[k, t, rank:] = grad.astype(BF16)
        recv = rs.at[RANK + k * SECOND]
        peers("t", lambda p: remote(RANK, "t", pbuf.at[k, t], pbuf.at[k, t], p, recv).start())

    low_t, grad_t = [], []

    def block_gradients(k):
        arrived(RANK + k * SECOND, "t", pbuf.at[k])
        total = pbuf[k, 0].astype(F32)
        for j in range(1, nt):
            total = total + pbuf[k, j].astype(F32)
        low_k, grad_k = total[:rank].astype(BF16), total[rank:].astype(BF16)
        low_t.append(low_k)
        grad_t.append(grad_k)
        span = slice(k * BLOCK, (k + 1) * BLOCK)
        g1[k, :, :first] = jnp.dot(grad_k, xv[span, :first], preferred_element_type=F32).astype(BF16)
        g1[k, :, first:] = (
            ADAPTER_SCALE * jnp.dot(low_k, vbuf[t, span, :], preferred_element_type=F32)
        ).astype(BF16)
        g2[k] = jnp.dot(grad_k, xv[span, first:], preferred_element_type=F32).astype(BF16)
        recv_z, recv_y = rs.at[GZ + k * SECOND], rs.at[GY + k * SECOND]
        peers("z", lambda p: remote(GZ, "z", g1.at[k], gz_v.at[k, z], p, recv_z).start())
        peers("y", lambda p: remote(GY, "y", g2.at[k], gy_v.at[k, y], p, recv_y).start())
        gz_v[k, z] = g1[k]
        gy_v[k, y] = g2[k]

    rank_products(0)
    for p in near_weights[1::2]:
        weight_to(p, 1, 4).start()
    rank_products(1)
    for part in range(2, 4):
        for p in near_weights[1::2]:
            weight_to(p, part, 4).start()
    for off in far + near:
        value_to(2 * chip(off) + core).start()
    forward(t).start()
    block_gradients(0)
    block_gradients(1)

    if count_shared:
        all_of("t", wbuf.at[pl.ds(0, count_shared), pl.ds(0, rows_half)], rs.at[SHARE]).wait_recv()
    for off in far:
        halves(chip(off))
    for off in far:
        send_base(chip(off))

    def add_up(k, p, owner, ten, buf, acc):
        total = acc[p]
        for j in range(buf.shape[1]):
            hit = jnp.where(ten[j, 0, k] == owner, 1.0, 0.0).astype(F32)
            total = total + hit * buf[k, j].astype(F32)
        return total

    def add1(k, p):
        return add_up(k, p, p * nz + z, tz_s, gz_v, acc1)

    def add2(k, p):
        return add_up(k, p, y * nz + p, ty_s, gy_v, acc2)

    acc1[...] = jnp.zeros_like(acc1)
    acc2[...] = jnp.zeros_like(acc2)
    for k in range(nb - 1):
        arrived(GZ + k * SECOND, "z", gz_v.at[k])
        arrived(GY + k * SECOND, "y", gy_v.at[k])

        def keep1(p, carry):
            acc1[p] = add1(k, p)
            return carry

        def keep2(p, carry):
            acc2[p] = add2(k, p)
            return carry

        lax.fori_loop(0, ny, keep1, 0)
        lax.fori_loop(0, nz, keep2, 0)

    for p in near_weights[1::2]:
        weight_arrived(p)
    for off in near:
        halves(chip(off))
    last = nb - 1

    def send_sum1(p):
        h1[p] = add1(last, p).astype(BF16)
        remote(HY, "y", h1.at[p], hz1.at[y], p).start()

    def send_sum2(p):
        h2[p] = add2(last, p).astype(BF16)
        remote(HZ, "z", h2.at[p], hz2.at[z], p).start()

    arrived(GZ + last * SECOND, "z", gz_v.at[last])
    peers("y", send_sum1)
    arrived(GY + last * SECOND, "y", gy_v.at[last])
    peers("z", send_sum2)
    hz1[y] = add1(last, y).astype(BF16)
    hz2[z] = add2(last, z).astype(BF16)
    for off in near:
        send_base(chip(off))

    if far + near:
        all_of("t", vbuf.at[pl.ds(0, nx - 1)], rs.at[VAL]).wait_recv()
    for off in far + near:
        forward(2 * chip(off) + core).start()
    for k in range(nb):
        span = slice(k * BLOCK, (k + 1) * BLOCK)
        gin_acc[span, :first] = tn_dot(grad_t[k], first_at[k])
        gin_acc[span, first:] = tn_dot(grad_t[k], second_at[k])
    all_of("t", vbuf.at[pl.ds(0, nx)], rs.at[FWD]).wait_recv()
    tiles = 4
    width = feats // tiles
    for i in range(tiles):
        cols = slice(i * width, (i + 1) * width)
        acc = gin_acc[:, cols]
        for j in range(nt):
            acc = acc + nt_dot(vbuf[j], wbuf[j, cols, :])
        gin_v[:, cols] = acc.astype(BF16)
    gin_out = pltpu.make_async_copy(gin_v, gin_hbm, loc.at[0])
    gin_out.start()

    arrived(CNT, "y", all_ten)
    local[7].wait()
    hits = jnp.where(all_ten[:, :, 0, :] == d, 1.0, 0.0).astype(F32)
    count = jnp.sum(hits) * BLOCK
    quota = jnp.full((8, 128), quo_s[d], jnp.int32).astype(F32)
    scale = (quota / jnp.maximum(jnp.full((8, 128), count, F32), 1.0))[:1, :1]
    arrived(HY, "y", hz1)
    acc = hz1[0].astype(F32)
    for j in range(1, ny):
        acc = acc + hz1[j].astype(F32)
    da_v[:, :first] = acc[:, :first] * scale
    db_v[...] = acc[:, first:] * scale
    up_out = pltpu.make_async_copy(db_v, db_hbm, loc.at[2])
    up_out.start()
    arrived(HZ, "z", hz2)
    acc = hz2[0].astype(F32)
    for j in range(1, nz):
        acc = acc + hz2[j].astype(F32)
    da_v[:, first:] = acc * scale
    down_out = pltpu.make_async_copy(da_v, da_hbm, loc.at[3])
    down_out.start()

    base = both(x)
    if far + near:
        all_of("t", ebuf.at[pl.ds(0, nx - 1)], rs.at[BASE]).wait_recv()
    for off in far + near:
        base = base + ebuf[chip(off)].astype(F32)
    for k in range(nb):
        span = slice(k * BLOCK, (k + 1) * BLOCK)
        raised = tn_dot(low_t[k], up_at[k])
        out_v[span, :] = (base[span] + ADAPTER_SCALE * raised).astype(BF16)

    value_out = pltpu.make_async_copy(out_v, out_hbm, loc.at[1])
    value_out.start()

    left(TZ, "z", tz_v)
    left(TY, "y", ty_v)
    left(AZ, "z", row1)
    left(AY, "y", col2)
    left(CNT, "y", all_ten)
    for k in range(1, nb):
        left(SY2, "y", s1.at[k])
        left(SZ2, "z", s2.at[k])
    left_both(RANK, "t", pbuf)
    left_both(GZ, "z", gz_v)
    left_both(GY, "y", gy_v)
    left(WGT, "t", wbuf, 1 + len(near_weights[1::2]))
    for kind in (WGT, SHARE):
        if count_shared:
            all_of("t", wbuf.at[pl.ds(0, count_shared), pl.ds(0, rows_half)], rs.at[0], kind).wait_send()
    left(VAL, "t", vbuf, nx - 1)
    left(FWD, "t", vbuf, nx)
    left(PRE, "t", presend, nx)
    left(BASE, "t", bsend, nx - 1)
    left(HY, "y", h1)
    left(HZ, "z", h2)
    for copy in (gin_out, value_out, up_out, down_out):
        copy.wait()


def write_out(out_v, gin_v, da_v, db_v, out_hbm, gin_hbm, da_hbm, db_hbm, sems):
    pairs = ((gin_v, gin_hbm), (out_v, out_hbm), (da_v, da_hbm), (db_v, db_hbm))
    copies = [pltpu.make_async_copy(a, b, sems.at[i]) for i, (a, b) in enumerate(pairs)]
    for copy in copies:
        copy.start()
    for copy in copies:
        copy.wait()


def solution(mesh):
    nt = mesh.shape["tensor"]
    nz = LINE
    ny = mesh.shape["dp"] // nz

    def on_device(x, w, a, b, v, tenants, quotas):
        rows, feats = x.shape
        values = v.shape[1]
        _, rank, _ = b.shape
        nb = tenants.shape[0]
        first = feats // 2
        wide, half = first + values, feats - first
        hbm = pl.BlockSpec(memory_space=pltpu.MemorySpace.HBM)
        anywhere = pl.BlockSpec(memory_space=pl.ANY)
        out, gin, da, db = pl.pallas_call(
            functools.partial(kernel, nt, ny, nz),
            out_shape=(
                jax.ShapeDtypeStruct((rows, values), BF16),
                jax.ShapeDtypeStruct((rows, feats), BF16),
                jax.ShapeDtypeStruct((rank, feats), F32),
                jax.ShapeDtypeStruct((rank, values), F32),
            ),
            in_specs=[hbm] * 7,
            out_specs=(anywhere,) * 4,
            scratch_shapes=[
                pltpu.VMEM((rows, values), BF16),
                pltpu.VMEM((rows, feats), BF16),
                pltpu.VMEM((rank, feats), F32),
                pltpu.VMEM((rank, values), F32),
                pltpu.SMEM((nb,), jnp.int32),
                pltpu.SMEM(quotas.shape, jnp.int32),
                pltpu.VMEM((1, 128), jnp.int32),
                pltpu.VMEM((nz, 1, 128), jnp.int32),
                pltpu.VMEM((ny, 1, 128), jnp.int32),
                pltpu.SMEM((nz, 1, 128), jnp.int32),
                pltpu.SMEM((ny, 1, 128), jnp.int32),
                pltpu.VMEM((ny, nz, 1, 128), jnp.int32),
                pltpu.VMEM((rows, feats), BF16),
                pltpu.VMEM((nz, rank, wide), BF16),
                pltpu.VMEM((ny, rank, half), BF16),
                pltpu.VMEM((nb, ny, rank, wide), BF16),
                pltpu.VMEM((nb, nz, rank, half), BF16),
                pltpu.VMEM((ny, rank, wide), BF16),
                pltpu.VMEM((ny, rank, wide), BF16),
                pltpu.VMEM((nz, rank, half), BF16),
                pltpu.VMEM((nz, rank, half), BF16),
                pltpu.VMEM((nt, rows, values), BF16),
                pltpu.VMEM((nt, feats, values), BF16),
                pltpu.VMEM((nb, nt, 2 * rank, BLOCK), BF16),
                pltpu.VMEM((nt // 2, rows, values), BF16),
                pltpu.VMEM((nt // 2, rows, values), BF16),
                pltpu.VMEM((nt // 2, rows, values), F32),
                pltpu.VMEM((nt // 2, rows, values), BF16),
                pltpu.VMEM((nt // 2, rows, values), BF16),
                pltpu.VMEM((nb, rank, wide), BF16),
                pltpu.VMEM((nb, rank, half), BF16),
                pltpu.VMEM((nb, nz, rank, wide), BF16),
                pltpu.VMEM((nb, ny, rank, half), BF16),
                pltpu.VMEM((ny, rank, wide), F32),
                pltpu.VMEM((nz, rank, half), F32),
                pltpu.VMEM((ny, rank, wide), BF16),
                pltpu.VMEM((nz, rank, half), BF16),
                pltpu.VMEM((ny, rank, wide), BF16),
                pltpu.VMEM((nz, rank, half), BF16),
                pltpu.VMEM((rows, feats), F32),
                pltpu.SemaphoreType.DMA((8,)),
                pltpu.SemaphoreType.DMA((SZ2 + 1,)),
                pltpu.SemaphoreType.DMA((KINDS,)),
                pltpu.SemaphoreType.DMA((nt,)),
                pltpu.SemaphoreType.DMA((nt // 2,)),
            ],
            compiler_params=pltpu.CompilerParams(
                collective_id=0, has_side_effects=True, vmem_limit_bytes=48 << 20
            ),
        )(*[
            pltpu.with_memory_space_constraint(arg, pltpu.MemorySpace.HBM)
            for arg in (tenants, quotas, x, w, jnp.swapaxes(a[0], 0, 1), b[0], v)
        ])
        out, gin, da, db = pl.pallas_call(
            write_out,
            out_shape=(
                jax.ShapeDtypeStruct((rows, values), BF16),
                jax.ShapeDtypeStruct((rows, feats), BF16),
                jax.ShapeDtypeStruct((rank, feats), F32),
                jax.ShapeDtypeStruct((rank, values), F32),
            ),
            in_specs=[anywhere] * 4,
            out_specs=(hbm,) * 4,
            scratch_shapes=[pltpu.SemaphoreType.DMA((4,))],
            compiler_params=pltpu.CompilerParams(vmem_limit_bytes=4 << 20),
        )(out, gin, da, db)
        return out, gin, jnp.swapaxes(da, 0, 1)[None], db[None]

    return jax.shard_map(
        on_device,
        mesh=mesh,
        in_specs=(
            P("dp", "tensor"),
            P(None, "tensor"),
            P("dp", "tensor", None),
            P("dp", None, "tensor"),
            P("dp", "tensor"),
            P("dp"),
            P(),
        ),
        out_specs=(
            P("dp", "tensor"),
            P("dp", "tensor"),
            P("dp", "tensor", None),
            P("dp", None, "tensor"),
        ),
        check_vma=False,
    )
```

time: 58.8 us -> 49.6 us (0.84); the launches traced: 57.7 us -> 49.5 us
  Pallas kernels: 57.1 us -> 48.9 us
    pallas_call x1, Pallas kernels: 56.2 us -> 48 us  [on_device(): pl.pallas_call(functools.partial(kernel, nt, ny, nz), out_shape=(jax.Shap...]
where the time goes in v3:
time: 49.6 us; the launch traced here: 49.5 us
  Pallas kernels  48.9 us (99%)
  between operations  0.64 us (1%)
    pallas_call x1, Pallas kernels, on_device(): pl.pallas_call(functools.partial(kernel, nt, ny, nz), out_shape=(jax.Shap...  48 us

profile of v3, /device:TPU:1, one launch (start us, length us, event | category | flops | bytes accessed | tf_op | source)
XLA Modules:
  0.0 49.5 jit_solution(10766684955166040746)
XLA Ops:
  0.6 48.0 %shard_map.102 = (bf16[256,128]{1,0:T(8,128)(2,1)S(1)}, bf16[256,1024]{1,0:T(8,128)(2,1)S(1)}, f32[16,1024]{1,0:T(8,128)S(1)}, f32[16,128]{1,0:T(8,128)S(1)}) custom-call(s32[2]{0:T(128)} %ten_hbm.1, s32[64]{0:T(128)} %quo_hbm.1, bf16[256,1024]{1,0:T(8,128)(2,1)} %x_hbm.1, bf16[8192,128]{1,0:T(8,128)(2,1)} %w_hbm.1, bf16[16,1024]{1,0:T(8,128)(2,1)} %bitcast.8, ...), custom_call_target="tpu_custom_call" | custom-call | tf_op jit(solution)/shard_map/pallas_call | solution.py:493
  48.6 0.9 %shard_map.103 = (bf16[256,128]{1,0:T(8,128)(2,1)}, bf16[256,1024]{1,0:T(8,128)(2,1)}, f32[16,1024]{1,0:T(8,128)}, f32[16,128]{1,0:T(8,128)}) custom-call(bf16[256,128]{1,0:T(8,128)(2,1)S(1)} %get-tuple-element.12.out_v, bf16[256,1024]{1,0:T(8,128)(2,1)S(1)} %get-tuple-element.13.gin_v, f32[16,1024]{1,0:T(8,128)S(1)} %get-tuple-element.14.da_v, ...), custom_call_target="tpu_custom_call" | custom-call | tf_op jit(solution)/shard_map/pallas_call | solution.py:557

commit v4 on v3

--- a/solution.py
+++ b/solution.py
@@ -14,8 +14,8 @@
 BF16 = jnp.bfloat16
 F32 = jnp.float32
 
-TZ, TY, AZ, AY, VAL, FWD, BASE, HY, HZ, CNT, SY, SZ, RANK, GZ, GY, WGT, PRE, SHARE, SY2, SZ2 = range(20)
-SECOND = 10
+TZ, TY, AZ, AY, VAL, FWD, BASE, HY, HZ, CNT, SY, SZ, RANK, GZ, GY, WGT, PRE, SHARE, SY2, SZ2, GZ2, GY2 = range(22)
+SECOND = 12
 KINDS = SECOND + GY + 1
 
 
@@ -52,6 +52,9 @@
     r1, r2 = (r1_first, r1_second), (r2_first, r2_second)
     first = feats - half
     values = v_hbm.shape[1]
+    wide = first + values
+    cut1, cut2 = pl.cdiv(wide, 256) * 128, half // 2
+    parts1, parts2 = (pl.ds(0, cut1), pl.ds(cut1, wide - cut1)), (pl.ds(0, cut2), pl.ds(cut2, half - cut2))
 
     lines = {
         "t": (t, nt, lambda p: {"tensor": p}),
@@ -76,6 +79,11 @@
         others = lines[line][1] - 1
         if others:
             all_of(line, buf.at[pl.ds(0, others)], rs.at[kind]).wait_recv()
+
+    def part_arrived(kind, line, buf, part):
+        others = lines[line][1] - 1
+        if others:
+            all_of(line, buf.at[pl.ds(0, others), :, part], rs.at[kind]).wait_recv()
 
     def left(kind, line, buf, copies=None):
         others = lines[line][1] - 1 if copies is None else copies
@@ -125,16 +133,14 @@
     tile[...] = mine
     tz_v[z] = mine
     ty_v[y] = mine
+    for copy in local[1:4]:
+        copy.wait()
     pl.semaphore_wait(barrier, nt + ny + nz - 3)
-
-    def adapter_to_z(p):
-        remote(AZ, "z", a_hbm.at[:, pl.ds(0, first)], row1.at[z, :, pl.ds(0, first)], p).start()
-        remote(AZ, "z", b_hbm, row1.at[z, :, pl.ds(first, values)], p).start()
 
     peers("z", lambda p: remote(TZ, "z", tile, tz_v.at[z], p).start())
     peers("y", lambda p: remote(TY, "y", tile, ty_v.at[y], p).start())
-    peers("z", adapter_to_z)
-    peers("y", lambda p: remote(AY, "y", a_hbm.at[:, pl.ds(first, half)], col2.at[y], p).start())
+    peers("z", lambda p: remote(AZ, "z", row1.at[z], row1.at[z], p).start())
+    peers("y", lambda p: remote(AY, "y", col2.at[y], col2.at[y], p).start())
 
     near = [off for off in range(1, nx) if min(off, nx - off) == 1]
     far = [off for off in range(1, nx) if off not in near]
@@ -187,8 +193,6 @@
     all_ten[y] = tz_v[...]
     to_z.wait()
     to_y.wait()
-    for copy in local[1:4]:
-        copy.wait()
 
     def pick1(k, p):
         return row1[lax.rem(ty_s[p, 0, k], nz)]
@@ -308,9 +312,14 @@
             ADAPTER_SCALE * jnp.dot(low_k, vbuf[t, span, :], preferred_element_type=F32)
         ).astype(BF16)
         g2[k] = jnp.dot(grad_k, xv[span, first:], preferred_element_type=F32).astype(BF16)
-        recv_z, recv_y = rs.at[GZ + k * SECOND], rs.at[GY + k * SECOND]
-        peers("z", lambda p: remote(GZ, "z", g1.at[k], gz_v.at[k, z], p, recv_z).start())
-        peers("y", lambda p: remote(GY, "y", g2.at[k], gy_v.at[k, y], p, recv_y).start())
+        kinds_z, kinds_y = (GZ + k * SECOND, GZ2), (GY + k * SECOND, GY2)
+        whole = k < nb - 1
+        for at1, at2, kz, ky in zip(
+            (pl.ds(0, wide),) if whole else parts1, (pl.ds(0, half),) if whole else parts2, kinds_z, kinds_y
+        ):
+            recv_z, recv_y = rs.at[kz], rs.at[ky]
+            peers("z", lambda p: remote(GZ, "z", g1.at[k, :, at1], gz_v.at[k, z, :, at1], p, recv_z).start())
+            peers("y", lambda p: remote(GY, "y", g2.at[k, :, at2], gy_v.at[k, y, :, at2], p, recv_y).start())
         gz_v[k, z] = g1[k]
         gy_v[k, y] = g2[k]
 
@@ -334,18 +343,18 @@
     for off in far:
         send_base(chip(off))
 
-    def add_up(k, p, owner, ten, buf, acc):
-        total = acc[p]
+    def add_up(k, p, owner, ten, buf, acc, part):
+        total = acc[p, :, part]
         for j in range(buf.shape[1]):
             hit = jnp.where(ten[j, 0, k] == owner, 1.0, 0.0).astype(F32)
-            total = total + hit * buf[k, j].astype(F32)
+            total = total + hit * buf[k, j, :, part].astype(F32)
         return total
 
-    def add1(k, p):
-        return add_up(k, p, p * nz + z, tz_s, gz_v, acc1)
-
-    def add2(k, p):
-        return add_up(k, p, y * nz + p, ty_s, gy_v, acc2)
+    def add1(k, p, part=slice(None)):
+        return add_up(k, p, p * nz + z, tz_s, gz_v, acc1, part)
+
+    def add2(k, p, part=slice(None)):
+        return add_up(k, p, y * nz + p, ty_s, gy_v, acc2, part)
 
     acc1[...] = jnp.zeros_like(acc1)
     acc2[...] = jnp.zeros_like(acc2)
@@ -370,18 +379,19 @@
         halves(chip(off))
     last = nb - 1
 
-    def send_sum1(p):
-        h1[p] = add1(last, p).astype(BF16)
-        remote(HY, "y", h1.at[p], hz1.at[y], p).start()
-
-    def send_sum2(p):
-        h2[p] = add2(last, p).astype(BF16)
-        remote(HZ, "z", h2.at[p], hz2.at[z], p).start()
-
-    arrived(GZ + last * SECOND, "z", gz_v.at[last])
-    peers("y", send_sum1)
-    arrived(GY + last * SECOND, "y", gy_v.at[last])
-    peers("z", send_sum2)
+    def send_sum1(p, part):
+        h1[p, :, part] = add1(last, p, part).astype(BF16)
+        remote(HY, "y", h1.at[p, :, part], hz1.at[y, :, part], p).start()
+
+    def send_sum2(p, part):
+        h2[p, :, part] = add2(last, p, part).astype(BF16)
+        remote(HZ, "z", h2.at[p, :, part], hz2.at[z, :, part], p).start()
+
+    for at1, at2, kz, ky in zip(parts1, parts2, (GZ + last * SECOND, GZ2), (GY + last * SECOND, GY2)):
+        part_arrived(kz, "z", gz_v.at[last], at1)
+        peers("y", lambda p: send_sum1(p, at1))
+        part_arrived(ky, "y", gy_v.at[last], at2)
+        peers("z", lambda p: send_sum2(p, at2))
     hz1[y] = add1(last, y).astype(BF16)
     hz2[z] = add2(last, z).astype(BF16)
     for off in near:

time: 49.6 us -> 49.1 us (0.990)
  Pallas kernels: 48.9 us -> 48.3 us
    pallas_call x1, Pallas kernels: 48 us -> 47.5 us  [on_device(): pl.pallas_call(functools.partial(kernel, nt, ny, nz), out_shape=(jax.Shap...]
where the time goes in v4:
time: 49.1 us; the launch traced here: 49 us
  Pallas kernels  48.3 us (98%)
  between operations  0.64 us (1%)
    pallas_call x1, Pallas kernels, on_device(): pl.pallas_call(functools.partial(kernel, nt, ny, nz), out_shape=(jax.Shap...  47.5 us

profile of v4, /device:TPU:1, one launch (start us, length us, event | category | flops | bytes accessed | tf_op | source)
XLA Modules:
  0.0 49.0 jit_solution(576019400882401586)
XLA Ops:
  0.6 47.5 %shard_map.102 = (bf16[256,128]{1,0:T(8,128)(2,1)S(1)}, bf16[256,1024]{1,0:T(8,128)(2,1)S(1)}, f32[16,1024]{1,0:T(8,128)S(1)}, f32[16,128]{1,0:T(8,128)S(1)}) custom-call(s32[2]{0:T(128)} %ten_hbm.1, s32[64]{0:T(128)} %quo_hbm.1, bf16[256,1024]{1,0:T(8,128)(2,1)} %x_hbm.1, bf16[8192,128]{1,0:T(8,128)(2,1)} %w_hbm.1, bf16[16,1024]{1,0:T(8,128)(2,1)} %bitcast.8, ...), custom_call_target="tpu_custom_call" | custom-call | tf_op jit(solution)/shard_map/pallas_call | solution.py:503
  48.1 0.9 %shard_map.103 = (bf16[256,128]{1,0:T(8,128)(2,1)}, bf16[256,1024]{1,0:T(8,128)(2,1)}, f32[16,1024]{1,0:T(8,128)}, f32[16,128]{1,0:T(8,128)}) custom-call(bf16[256,128]{1,0:T(8,128)(2,1)S(1)} %get-tuple-element.12.out_v, bf16[256,1024]{1,0:T(8,128)(2,1)S(1)} %get-tuple-element.13.gin_v, f32[16,1024]{1,0:T(8,128)S(1)} %get-tuple-element.14.da_v, ...), custom_call_target="tpu_custom_call" | custom-call | tf_op jit(solution)/shard_map/pallas_call | solution.py:567
